TPU v7x, 32 devices: a whole 2x2x4 slice. The times are simulated.
32 devices in a mesh: expert: 8 (over y, x, core), section: 4 (over z).
Axes of the slice: x: 2, y: 2, z: 4, core: 2. Of those that a mesh axis runs over, the one named last changes fastest.
Arguments:
- rows_in: bfloat16 [8, 512, 3072], P('expert', 'section'), may hold values from -6 to 6
- route_prob: float32 [8, 512], P('expert', 'section'), may hold values from 0.2 to 1
- w_in: bfloat16 [8, 128, 8, 3072], P('expert', 'section'), may hold values from -0.109375 to 0.109375
- w_down: bfloat16 [8, 128, 4, 3072], P('expert', 'section'), may hold values from -0.5 to 0.5
- m_send: float32 [8, 48, 3072], P('expert', 'section'), may hold values from -6 to 6
- v_send: float32 [8, 48, 3072], P('expert', 'section'), may hold values from 0.01 to 1
- chosen: int32 [8, 4], P('expert', 'section'), may hold values from 0 to 31
- swap_mask: int32 [4], P('section'), may hold values from 1 to 7, as said below
- dest_slot: int32 [8, 512], P('expert', 'section'), may hold values from 0 to 7, as said below
- dest_row: int32 [8, 512], P('expert', 'section'), may hold values from 0 to 191, as said below
Outputs:
- routed: bfloat16 [8, 768, 3072], P('expert', 'section')
- m_recv: float32 [8, 48, 3072], P('expert', 'section')
- v_recv: float32 [8, 48, 3072], P('expert', 'section')
Inputs may be any that keep to these rules, and one draw needn't show every extreme that they name: `swap_mask`: the mask of one section sets every bit of a slot index. `dest_slot`: among the rows of one slot, at most 32 go to one slot of the next section, and one slot of the next section receives 192 rows in all; no slot receives more. `dest_row`: rows arriving at one slot of the next section have distinct destination rows.
All inputs are finite; a program needn't handle non-finite values.
Results may differ from a plain program's by a relative error of at most 0.0049.
Values may be sent and summed in bfloat16 or wider, within the bound.
No kernel may reach another device: no remote copies, remote signals or barrier semaphores. Data moves between devices by JAX's collectives and lax.ppermute only.
A program may use at most 64 MiB of HBM per device.

v0:
```python
import jax
import jax.numpy as jnp
from jax import lax
from jax.sharding import PartitionSpec as P


def from_partner(x, axis, apart):
    return lax.ppermute(x, axis, [(i, i ^ 1 << apart) for i in range(lax.axis_size(axis))])


def passed_along(block, axis, distance):
    devices = range(lax.axis_size(axis))
    route = [((i - distance) % len(devices), i) for i in devices]
    return lax.ppermute(block, axis, route)


def place_rows(arrived_rows, arrived_labels, out_rows):
    model_width = arrived_rows.shape[-1]
    buffer = jnp.zeros((out_rows, model_width), jnp.bfloat16)
    return buffer.at[arrived_labels.reshape(-1)].set(
        arrived_rows.reshape(-1, model_width), mode="drop"
    )


def pack_rows(expert_rows, target, landing, peer_count, capacity, out_rows):
    model_width = expert_rows.shape[-1]
    onehot = (target[:, None] == jnp.arange(peer_count, dtype=jnp.int32)[None, :]).astype(jnp.int32)
    position = jnp.sum((jnp.cumsum(onehot, 0) - onehot) * onehot, 1)
    packed = (
        jnp.zeros((peer_count, capacity, model_width), jnp.bfloat16)
        .at[target, position]
        .set(expert_rows)
    )
    labels = jnp.full((peer_count, capacity), out_rows, jnp.int32).at[target, position].set(landing)
    return (packed, labels)


def per_device(
    rows_in, route_prob, w_in, w_down, m_send, v_send, chosen, swap_mask, dest_slot, dest_row
):
    panels = w_in.shape[1]
    unit_count = w_down.shape[2]
    model_width = w_in.shape[3]
    chosen_panel = chosen[0, 0]
    pair_mask = swap_mask[0]
    given_in = lax.dynamic_index_in_dim(w_in[0], chosen_panel, 0, keepdims=False)
    given_down = lax.dynamic_index_in_dim(w_down[0], chosen_panel, 0, keepdims=False)
    levels = lax.axis_size("expert").bit_length() - 1
    bit_list = list(range(levels))
    weights = jnp.concatenate([given_in, given_down], 0)
    moments = jnp.stack([m_send[0], v_send[0]], 0)
    for bit_number in bit_list:
        arrived_w = from_partner(weights, "expert", bit_number)
        arrived_m = from_partner(moments, "expert", bit_number)
        bit_flag = jnp.bitwise_and(jnp.right_shift(pair_mask, bit_number), 1) == 1
        weights = jnp.where(bit_flag, arrived_w, weights)
        moments = jnp.where(bit_flag, arrived_m, moments)
    slot_hit = (jnp.arange(panels, dtype=jnp.int32) == chosen_panel)[:, None, None]
    new_in = jnp.where(slot_hit, weights[None, : 2 * unit_count], w_in[0])
    new_down = jnp.where(slot_hit, weights[None, 2 * unit_count :], w_down[0])
    gate_w = new_in[:, :unit_count].reshape(panels * unit_count, model_width)
    up_w = new_in[:, unit_count:].reshape(panels * unit_count, model_width)
    down_w = new_down.reshape(panels * unit_count, model_width)
    tokens = rows_in[0]
    contract_dims = (((1,), (1,)), ((), ()))
    gate_pre = lax.dot_general(tokens, gate_w, contract_dims, preferred_element_type=jnp.float32)
    up_pre = lax.dot_general(tokens, up_w, contract_dims, preferred_element_type=jnp.float32)
    hidden = (jax.nn.silu(gate_pre) * up_pre).astype(jnp.bfloat16)
    mixed = jnp.dot(hidden, down_w, preferred_element_type=jnp.float32)
    expert_rows = (route_prob[0][:, None] * mixed).astype(jnp.bfloat16)
    peer_count = lax.axis_size("expert")
    row_count = tokens.shape[0]
    capacity = 2 * row_count // peer_count
    out_rows = row_count + row_count // 2
    moved_rows, moved_slot, moved_place = passed_along(
        (expert_rows, dest_slot[0], dest_row[0]), "section", 1
    )
    packed, labels = pack_rows(moved_rows, moved_slot, moved_place, peer_count, capacity, out_rows)
    arrived_rows, arrived_labels = (
        lax.all_to_all(packed, "expert", split_axis=0, concat_axis=0, tiled=True),
        lax.all_to_all(labels, "expert", split_axis=0, concat_axis=0, tiled=True),
    )
    routed = place_rows(arrived_rows, arrived_labels, out_rows)
    return (routed[None], moments[0][None], moments[1][None])


def solution(mesh):
    in_specs = (
        P("expert", "section", None),
        P("expert", "section"),
        P("expert", "section", None, None),
        P("expert", "section", None, None),
        P("expert", "section", None),
        P("expert", "section", None),
        P("expert", "section"),
        P("section"),
        P("expert", "section"),
        P("expert", "section"),
    )
    out_specs = (
        P("expert", "section", None),
        P("expert", "section", None),
        P("expert", "section", None),
    )
    return jax.shard_map(
        per_device, mesh=mesh, in_specs=in_specs, out_specs=out_specs, check_vma=False
    )
```

profile of v0, /device:TPU:0, one launch (start us, length us, event | category | flops | bytes accessed | tf_op | source)
XLA Modules:
  0.0 111.3 jit_solution(18313368867725388079)
XLA Ops:
  0.6 0.0 copy-start
  1.4 0.8 dynamic-slice_bitcast_fusion
  2.2 0.7 dynamic-slice_bitcast_fusion.1
  2.9 0.5 collective-permute-start.2
  3.5 2.6 %collective-permute-start = (s32[128]{0:T(128)}, s32[128]{0:T(128)S(1)}, u32[]{:S(2)}, u32[]{:S(2)}) collective-permute-start(s32[128]{0:T(128)} %bitcast.64), channel_id=1, source_target_pairs={{3,0},{0,1},{1,2},{2,3},{7,4},{4,5},{5,6},{6,7},{11,8},{8,9},{9,10... | collective-permute-start | bytes 1544 | tf_op jit(solution)/shard_map/ppermute | solution.py:14
  6.1 1.6 %collective-permute-start.1 = (s32[128]{0:T(128)}, s32[128]{0:T(128)S(1)}, u32[]{:S(2)}, u32[]{:S(2)}) collective-permute-start(s32[128]{0:T(128)} %bitcast.65), channel_id=1, source_target_pairs={{3,0},{0,1},{1,2},{2,3},{7,4},{4,5},{5,6},{6,7},{11,8},{8,9},{9,10... | collective-permute-start | bytes 1544 | tf_op jit(solution)/shard_map/ppermute | solution.py:14
  7.7 2.0 %pad_maximum_fusion = f32[2,12,3072]{2,0,1:T(2,128)} fusion(f32[1,12,3072]{2,0,1:T(1,128)} %param.15, f32[1,12,3072]{2,0,1:T(1,128)} %param.14), kind=kLoop, calls=%fused_computation.16 | loop fusion | flops 73728 | bytes 589824 | tf_op jit(solution)/shard_map/stack | solution.py:51
  9.7 1.6 %squeeze.36 = bf16[128,3072]{1,0:T(8,128)(2,1)S(1)} reshape(bf16[1,32,4,3072]{3,2,1,0:T(4,128)(2,1)} %param.13) | data formatting | bytes 1572864 | tf_op jit(solution)/shard_map/squeeze | solution.py:47
  11.9 0.1 broadcast_in_dim.68
  12.0 0.1 broadcast_in_dim.69
  12.1 1.6 %collective-permute-start.3 = (bf16[12,3072]{1,0:T(8,128)(2,1)S(1)}, bf16[12,3072]{1,0:T(8,128)(2,1)S(1)}, u32[]{:S(2)}, u32[]{:S(2)}) collective-permute-start(bf16[12,3072]{1,0:T(8,128)(2,1)S(1)} %broadcast_select_fusion.3), channel_id=1, source_target_pairs={{0,8},{4,12},{8,0},{12,4},{16,24},{20,28},{24,16},{28,20},{1,9},{5... | collective-permute-start | bytes 221192 | tf_op jit(solution)/shard_map/ppermute | solution.py:8
  13.7 0.1 fusion.15
  13.8 0.2 reduce_window_sum.11
  14.0 3.5 %collective-permute-done.3 = bf16[12,3072]{1,0:T(8,128)(2,1)S(1)} collective-permute-done((bf16[12,3072]{1,0:T(8,128)(2,1)S(1)}, bf16[12,3072]{1,0:T(8,128)(2,1)S(1)}, u32[]{:S(2)}, u32[]{:S(2)}) %collective-permute-start.3) | collective-permute-done | bytes 73760 | tf_op jit(solution)/shard_map/ppermute | solution.py:8
  17.4 1.6 %collective-permute-start.4 = (bf16[12,3072]{1,0:T(8,128)(2,1)S(1)}, bf16[12,3072]{1,0:T(8,128)(2,1)S(1)}, u32[]{:S(2)}, u32[]{:S(2)}) collective-permute-start(bf16[12,3072]{1,0:T(8,128)(2,1)S(1)} %broadcast_select_fusion.4), channel_id=1, source_target_pairs={{0,16},{4,20},{8,24},{12,28},{16,0},{20,4},{24,8},{28,12},{1,17},{... | collective-permute-start | bytes 221192 | tf_op jit(solution)/shard_map/ppermute | solution.py:8
  19.0 0.2 select_reduce_fusion
  19.2 2.9 %collective-permute-done.4 = bf16[12,3072]{1,0:T(8,128)(2,1)S(1)} collective-permute-done((bf16[12,3072]{1,0:T(8,128)(2,1)S(1)}, bf16[12,3072]{1,0:T(8,128)(2,1)S(1)}, u32[]{:S(2)}, u32[]{:S(2)}) %collective-permute-start.4) | collective-permute-done | bytes 73760 | tf_op jit(solution)/shard_map/ppermute | solution.py:8
  22.1 0.0 copy-start.5
  22.2 0.2 bitcast_select_fusion
  22.3 1.4 %fusion.21 = (bf16[32,4,3072]{2,1,0:T(4,128)(2,1)}, bf16[32,4,3072]{2,1,0:T(4,128)(2,1)S(1)}) fusion(bf16[32,8,3072]{2,1,0:T(8,128)(2,1)S(1)} %bitcast_select_fusion), kind=kLoop, calls=%fused_computation.46 | loop fusion | bytes 3145728 | tf_op jit(solution)/shard_map/slice | solution.py:61
  23.7 1.6 %reshape.97 = bf16[128,3072]{1,0:T(8,128)(2,1)S(1)} reshape(bf16[32,4,3072]{2,1,0:T(4,128)(2,1)} %get-tuple-element.3) | data formatting | bytes 1572864 | tf_op jit(solution)/shard_map/reshape | solution.py:61
  25.3 1.1 reshape.98
  26.4 0.2 broadcast_in_dim.71
  26.6 0.0 copy-start.3
  26.6 0.0 copy-start.4
  26.6 1.1 broadcast_in_dim.72
  27.7 0.4 convolution_bitcast_fusion.1
  28.1 0.0 collective-permute-done.6
  28.1 1.0 broadcast_select_fusion
  29.1 1.5 %collective-permute-start.7 = (f32[2,12,3072]{2,0,1:T(2,128)}, f32[2,12,3072]{2,0,1:T(2,128)}, u32[]{:S(2)}, u32[]{:S(2)}) collective-permute-start(f32[2,12,3072]{2,0,1:T(2,128)} %broadcast_select_fusion), channel_id=1, source_target_pairs={{0,8},{4,12},{8,0},{12,4},{16,24},{20,28},{24,16},{28,20},{1,9},{5... | collective-permute-start | bytes 884744 | tf_op jit(solution)/shard_map/ppermute | solution.py:8
  30.6 3.1 %fusion = bf16[128,3072]{1,0:T(8,128)(2,1)} fusion(bf16[128,3072]{1,0:T(8,128)(2,1)S(1)} %copy-done.1, bf16[1,128,3072]{2,1,0:T(8,128)(2,1)S(1)} %copy-done, bf16[128,3072]{1,0:T(8,128)(2,1)} %broadcast_in_dim.72, bf16[128,3072]{1,0:T(8,128)(2,1)S(1)} %squeeze.36, f32[128]{0:T(128)S(1)} %bitcast.63, pred[128]{0:T(512)(128)(4,1)S(1)} %broadcast_in_dim.69, ...), kind=kOutput, calls=%fused_computation.4 | convolution fusion | flops 202604544 | bytes 3998336 | tf_op jit(solution)/shard_map/dot_general | solution.py:69
  33.8 2.5 %collective-permute-start.5 = (bf16[128,3072]{1,0:T(8,128)(2,1)}, bf16[128,3072]{1,0:T(8,128)(2,1)S(1)}, u32[]{:S(2)}, u32[]{:S(2)}) collective-permute-start(bf16[128,3072]{1,0:T(8,128)(2,1)} %fusion), channel_id=1, source_target_pairs={{3,0},{0,1},{1,2},{2,3},{7,4},{4,5},{5,6},{6,7},{11,8},{8,9},{9,10... | collective-permute-start | bytes 2359304 | tf_op jit(solution)/shard_map/ppermute | solution.py:14
  36.3 0.6 collective-permute-done.7
  36.9 0.4 broadcast_select_fusion.1
  37.3 1.6 %collective-permute-start.8 = (f32[2,12,3072]{2,0,1:T(2,128)S(1)}, f32[2,12,3072]{2,0,1:T(2,128)S(1)}, u32[]{:S(2)}, u32[]{:S(2)}) collective-permute-start(f32[2,12,3072]{2,0,1:T(2,128)S(1)} %broadcast_select_fusion.1), channel_id=1, source_target_pairs={{0,16},{4,20},{8,24},{12,28},{16,0},{20,4},{24,8},{28,12},{1,17},{... | collective-permute-start | bytes 884744 | tf_op jit(solution)/shard_map/ppermute | solution.py:8
  38.9 0.0 collective-permute-done.1
  38.9 6.4 %scatter_fusion = s32[8,32]{1,0:T(8,128)S(1)} fusion(s32[8,32]{1,0:T(8,128)S(1)} %broadcast_in_dim.63, s32[128]{0:T(128)S(1)} %fusion.19, s32[128]{0:T(128)S(1)} %collective-permute-done.1), kind=kCustom, calls=%fused_computation | custom fusion | bytes 2560 | tf_op jit(solution)/shard_map/scatter | solution.py:34
  45.3 7.2 %all_to_all.14 = s32[8,1,32]{2,1,0:T(1,128)S(1)} all-to-all(s32[8,1,32]{2,1,0:T(1,128)S(1)} %bitcast.56), channel_id=1, replica_groups=mesh['expert'=8,'section'=4] {'expert'}, dimensions={0} | all-to-all | bytes 2048 | tf_op jit(solution)/shard_map/all_to_all | solution.py:81
  52.5 0.5 broadcast.103
  53.0 0.7 reduce.3
  53.7 0.1 reshape.96
  53.8 0.0 collective-permute-done.5
  53.8 1.3 %broadcast_in_dim.65 = bf16[8,32,3072]{2,1,0:T(8,128)(2,1)} broadcast(bf16[]{:T(256)} %constant.36.clone.1), dimensions={} | broadcast | bytes 1572866 | tf_op jit(solution)/shard_map/broadcast_in_dim | solution.py:30
  55.1 27.8 %scatter_fusion.1 = bf16[8,32,3072]{2,1,0:T(8,128)(2,1)} fusion(bf16[8,32,3072]{2,1,0:T(8,128)(2,1)} %broadcast_in_dim.65, s32[128]{0:T(128)S(1)} %fusion.19, bf16[128,3072]{1,0:T(8,128)(2,1)S(1)} %collective-permute-done.5), kind=kCustom, calls=%fused_computation.1 | custom fusion | bytes 2360320 | tf_op jit(solution)/shard_map/scatter | solution.py:32
  83.0 3.6 %all-to-all-start.1 = ((bf16[8,32,3072]{2,1,0:T(8,128)(2,1)}), bf16[8,32,3072]{2,1,0:T(8,128)(2,1)S(1)}, u32[]{:S(2)}, u32[]{:S(2)}) async-start(bf16[8,32,3072]{2,1,0:T(8,128)(2,1)} %scatter_fusion.1), calls=%async_computation.1 | async-start | bytes 3145728 | tf_op jit(solution)/shard_map/all_to_all | solution.py:80
  86.6 0.9 fusion.22
  87.5 20.0 %all-to-all-done.1 = bf16[8,32,3072]{2,1,0:T(8,128)(2,1)S(1)} async-done(((bf16[8,32,3072]{2,1,0:T(8,128)(2,1)}), bf16[8,32,3072]{2,1,0:T(8,128)(2,1)S(1)}, u32[]{:S(2)}, u32[]{:S(2)}) %all-to-all-start.1) | async-done | bytes 1572896 | tf_op jit(solution)/shard_map/all_to_all | solution.py:80
  107.5 3.8 %scatter_custom_fusion.2 = bf16[192,3072]{1,0:T(8,128)(2,1)} fusion(s32[256]{0:T(256)S(1)} %bitcast.62, bf16[256,3072]{1,0:T(8,128)(2,1)S(1)} %bitcast.57, bf16[]{:T(256)} %constant.36.clone.1), kind=kCustom, calls=%fused_computation.14 | custom fusion | bytes 1179650 | tf_op jit(solution)/shard_map/scatter | solution.py:20
  (26 shorter events, 0.2 us)
Async XLA Ops:
  0.6 27.1 %copy-start = (bf16[1,128,3072]{2,1,0:T(8,128)(2,1)S(1)}, bf16[1,128,3072]{2,1,0:T(8,128)(2,1)}, u32[]{:S(2)}) copy-start(bf16[1,128,3072]{2,1,0:T(8,128)(2,1)} %param.10) | copy-start | bytes 2359300
  2.9 9.1 %collective-permute-start.2 = (bf16[12,3072]{1,0:T(8,128)(2,1)S(1)}, bf16[12,3072]{1,0:T(8,128)(2,1)S(1)}, u32[]{:S(2)}, u32[]{:S(2)}) collective-permute-start(bf16[12,3072]{1,0:T(8,128)(2,1)S(1)} %pad_maximum_fusion.1), channel_id=1, source_target_pairs={{0,4},{4,0},{8,12},{12,8},{16,20},{20,16},{24,28},{28,24},{1,5},{5... | collective-permute-start | bytes 221192 | tf_op jit(solution)/shard_map/ppermute | solution.py:8
  3.5 10.2 %collective-permute-start = (s32[128]{0:T(128)}, s32[128]{0:T(128)S(1)}, u32[]{:S(2)}, u32[]{:S(2)}) collective-permute-start(s32[128]{0:T(128)} %bitcast.64), channel_id=1, source_target_pairs={{3,0},{0,1},{1,2},{2,3},{7,4},{4,5},{5,6},{6,7},{11,8},{8,9},{9,10... | collective-permute-start | bytes 1544 | tf_op jit(solution)/shard_map/ppermute | solution.py:14
  6.1 16.1 %copy-start.2 = (bf16[1,32,8,3072]{3,2,1,0:T(8,128)(2,1)S(1)}, bf16[1,32,8,3072]{3,2,1,0:T(8,128)(2,1)}, u32[]{:S(2)}) copy-start(bf16[1,32,8,3072]{3,2,1,0:T(8,128)(2,1)} %param.12) | copy-start | bytes 4718596
  6.1 32.8 %collective-permute-start.1 = (s32[128]{0:T(128)}, s32[128]{0:T(128)S(1)}, u32[]{:S(2)}, u32[]{:S(2)}) collective-permute-start(s32[128]{0:T(128)} %bitcast.65), channel_id=1, source_target_pairs={{3,0},{0,1},{1,2},{2,3},{7,4},{4,5},{5,6},{6,7},{11,8},{8,9},{9,10... | collective-permute-start | bytes 1544 | tf_op jit(solution)/shard_map/ppermute | solution.py:14
  9.7 18.4 %collective-permute-start.6 = (f32[2,12,3072]{2,0,1:T(2,128)}, f32[2,12,3072]{2,0,1:T(2,128)}, u32[]{:S(2)}, u32[]{:S(2)}) collective-permute-start(f32[2,12,3072]{2,0,1:T(2,128)} %pad_maximum_fusion), channel_id=1, source_target_pairs={{0,4},{4,0},{8,12},{12,8},{16,20},{20,16},{24,28},{28,24},{1,5},{5... | collective-permute-start | bytes 884744 | tf_op jit(solution)/shard_map/ppermute | solution.py:8
  12.1 5.3 %collective-permute-start.3 = (bf16[12,3072]{1,0:T(8,128)(2,1)S(1)}, bf16[12,3072]{1,0:T(8,128)(2,1)S(1)}, u32[]{:S(2)}, u32[]{:S(2)}) collective-permute-start(bf16[12,3072]{1,0:T(8,128)(2,1)S(1)} %broadcast_select_fusion.3), channel_id=1, source_target_pairs={{0,8},{4,12},{8,0},{12,4},{16,24},{20,28},{24,16},{28,20},{1,9},{5... | collective-permute-start | bytes 221192 | tf_op jit(solution)/shard_map/ppermute | solution.py:8
  17.4 4.7 %collective-permute-start.4 = (bf16[12,3072]{1,0:T(8,128)(2,1)S(1)}, bf16[12,3072]{1,0:T(8,128)(2,1)S(1)}, u32[]{:S(2)}, u32[]{:S(2)}) collective-permute-start(bf16[12,3072]{1,0:T(8,128)(2,1)S(1)} %broadcast_select_fusion.4), channel_id=1, source_target_pairs={{0,16},{4,20},{8,24},{12,28},{16,0},{20,4},{24,8},{28,12},{1,17},{... | collective-permute-start | bytes 221192 | tf_op jit(solution)/shard_map/ppermute | solution.py:8
  22.1 1.6 %copy-start.5 = (bf16[12,3072]{1,0:T(8,128)(2,1)}, bf16[12,3072]{1,0:T(8,128)(2,1)S(1)}, u32[]{:S(2)}) copy-start(bf16[12,3072]{1,0:T(8,128)(2,1)S(1)} %broadcast_select_fusion.5) | copy-start | bytes 221188
  23.7 2.7 %slice-start = ((bf16[12,3072]{1,0:T(8,128)(2,1)}), bf16[4,3072]{1,0:T(4,128)(2,1)S(1)}, s32[]{:S(2)}) async-start(bf16[12,3072]{1,0:T(8,128)(2,1)} %copy-done.5), calls=%async_computation.2 | async-start | bytes 49152 | tf_op jit(solution)/shard_map/slice | solution.py:60
  26.6 1.5 %copy-start.3 = (f32[1,12,3072]{2,0,1:T(1,128)S(1)}, f32[1,12,3072]{2,0,1:T(1,128)}, u32[]{:S(2)}) copy-start(f32[1,12,3072]{2,0,1:T(1,128)} %param.15) | copy-start | bytes 442372
  26.6 1.5 %copy-start.4 = (f32[1,12,3072]{2,0,1:T(1,128)S(1)}, f32[1,12,3072]{2,0,1:T(1,128)}, u32[]{:S(2)}) copy-start(f32[1,12,3072]{2,0,1:T(1,128)} %param.14) | copy-start | bytes 442372
  27.7 2.9 %copy-start.1 = (bf16[128,3072]{1,0:T(8,128)(2,1)S(1)}, bf16[128,3072]{1,0:T(8,128)(2,1)}, u32[]{:S(2)}) copy-start(bf16[128,3072]{1,0:T(8,128)(2,1)} %reshape.98) | copy-start | bytes 2359300
  27.7 2.9 %copy-start.6 = (f32[1,128]{1,0:T(1,128)S(1)}, f32[1,128]{1,0:T(1,128)}, u32[]{:S(2)}) copy-start(f32[1,128]{1,0:T(1,128)} %param.11) | copy-start | bytes 1540
  29.1 7.8 %collective-permute-start.7 = (f32[2,12,3072]{2,0,1:T(2,128)}, f32[2,12,3072]{2,0,1:T(2,128)}, u32[]{:S(2)}, u32[]{:S(2)}) collective-permute-start(f32[2,12,3072]{2,0,1:T(2,128)} %broadcast_select_fusion), channel_id=1, source_target_pairs={{0,8},{4,12},{8,0},{12,4},{16,24},{20,28},{24,16},{28,20},{1,9},{5... | collective-permute-start | bytes 884744 | tf_op jit(solution)/shard_map/ppermute | solution.py:8
  33.8 20.0 %collective-permute-start.5 = (bf16[128,3072]{1,0:T(8,128)(2,1)}, bf16[128,3072]{1,0:T(8,128)(2,1)S(1)}, u32[]{:S(2)}, u32[]{:S(2)}) collective-permute-start(bf16[128,3072]{1,0:T(8,128)(2,1)} %fusion), channel_id=1, source_target_pairs={{3,0},{0,1},{1,2},{2,3},{7,4},{4,5},{5,6},{6,7},{11,8},{8,9},{9,10... | collective-permute-start | bytes 2359304 | tf_op jit(solution)/shard_map/ppermute | solution.py:14
  37.3 49.2 %collective-permute-start.8 = (f32[2,12,3072]{2,0,1:T(2,128)S(1)}, f32[2,12,3072]{2,0,1:T(2,128)S(1)}, u32[]{:S(2)}, u32[]{:S(2)}) collective-permute-start(f32[2,12,3072]{2,0,1:T(2,128)S(1)} %broadcast_select_fusion.1), channel_id=1, source_target_pairs={{0,16},{4,20},{8,24},{12,28},{16,0},{20,4},{24,8},{28,12},{1,17},{... | collective-permute-start | bytes 884744 | tf_op jit(solution)/shard_map/ppermute | solution.py:8
  83.0 24.5 %all-to-all-start.1 = ((bf16[8,32,3072]{2,1,0:T(8,128)(2,1)}), bf16[8,32,3072]{2,1,0:T(8,128)(2,1)S(1)}, u32[]{:S(2)}, u32[]{:S(2)}) async-start(bf16[8,32,3072]{2,1,0:T(8,128)(2,1)} %scatter_fusion.1), calls=%async_computation.1 | async-start | bytes 3145728 | tf_op jit(solution)/shard_map/all_to_all | solution.py:80
where the time goes:
time: 113 us; the launch traced here: 111 us
  local copies, waits for them, and re-layouts  49.5 us (44%)
  waiting for transfers between devices  27 us (24%)
  starting transfers between devices  17.1 us (15%)
  blocking collectives  7.22 us (6%)
  other arithmetic  4.77 us (4%)
  matrix products  3.5 us (3%)
  between operations  2.25 us (2%)
    scatter x1, local copies, waits for them, and re-layouts, pack_rows(): packed = jnp.zeros((peer_count, capacity, model_width), jnp.bfloat16).at[...  27.8 us
    all_to_all x1, waiting for transfers between devices, per_device(): lax.all_to_all(packed, 'expert', split_axis=0, concat_axis=0, tiled=True)  20 us
    all_to_all x1, blocking collectives, per_device(): lax.all_to_all(labels, 'expert', split_axis=0, concat_axis=0, tiled=True)  7.22 us
    ppermute x6, waiting for transfers between devices, from_partner(): lax.ppermute(x, axis, [(i, i ^ 1 << apart) for i in range(lax.axis_size(a...  7.02 us
    ppermute x6, starting transfers between devices, from_partner(): lax.ppermute(x, axis, [(i, i ^ 1 << apart) for i in range(lax.axis_size(a...  6.75 us
    ppermute x3, starting transfers between devices, passed_along(): return lax.ppermute(block, axis, route)  6.75 us
    scatter x1, local copies, waits for them, and re-layouts, pack_rows(): jnp.full((peer_count, capacity), out_rows, jnp.int32).at[target, position]  6.37 us
    scatter x1, local copies, waits for them, and re-layouts, place_rows(): buffer.at[arrived_labels.reshape(-1)]  3.79 us
  transfers between devices with their start and end apart: 10, of which 4 were waited for; matrix products, arithmetic and copies ran while one was open for 47% of the time, Pallas kernels for 0%

commit v1 on v0

v1 whole, which is shorter than its diff:
```python
import jax
import jax.numpy as jnp
from jax import lax
from jax.sharding import PartitionSpec as P

LANES = 128


def exchange(arrays, axis, pair_mask):
    size = lax.axis_size(axis)
    low = 0
    while (1 << low) < size:
        bits = min(3, size.bit_length() - 1 - low)
        digit = jnp.bitwise_and(jnp.right_shift(pair_mask, low), (1 << bits) - 1)
        routes = [[(i, i ^ (k << low)) for i in range(size)] for k in range(1 << bits)]
        arms = [lambda held, r=r: [lax.ppermute(x, axis, r) for x in held] for r in routes[1:]]
        arrays = lax.switch(digit, [lambda held: list(held)] + arms, list(arrays))
        low += bits
    return arrays


def rows_times_rows(a, b):
    return lax.dot_general(a, b, (((1,), (1,)), ((), ())), preferred_element_type=jnp.float32)


def columns_times_columns(a, b):
    return lax.dot_general(a, b, (((0,), (0,)), ((), ())), preferred_element_type=jnp.float32)


def per_device(
    rows_in, route_prob, w_in, w_down, m_send, v_send, chosen, swap_mask, dest_slot, dest_row
):
    panels, units2, width = w_in.shape[1:]
    units = units2 // 2
    peers = lax.axis_size("expert")
    sections = lax.axis_size("section")
    tokens = rows_in[0]
    rows = tokens.shape[0]
    capacity = 2 * rows // peers
    out_rows = rows + rows // 2
    panel = chosen[0, 0]
    onward = [(i, (i + 1) % sections) for i in range(sections)]

    pre = rows_times_rows(tokens, w_in[0].reshape(panels * units2, width))
    column = jnp.arange(panels * units2)
    stays = (column % units2 < units) & (column // units2 != panel)
    hidden = jax.nn.silu(pre) * jnp.roll(pre, -units, 1)
    hidden = jnp.where(stays[None], hidden, 0).astype(jnp.bfloat16)
    down = jnp.pad(w_down[0], ((0, 0), (0, units), (0, 0))).reshape(panels * units2, width)
    mixed = jnp.dot(hidden, down, preferred_element_type=jnp.float32)
    base = (route_prob[0][:, None] * mixed).astype(jnp.bfloat16)

    given_in = lax.dynamic_index_in_dim(w_in[0], panel, 0, keepdims=False)
    given_down = lax.dynamic_index_in_dim(w_down[0], panel, 0, keepdims=False)
    given = jnp.concatenate([given_in, given_down], 0)
    base, given, m_held, v_held = lax.optimization_barrier((base, given, m_send[0], v_send[0]))
    arrived_base = lax.ppermute(base, "section", onward)
    taken, m_recv, v_recv = exchange([given, m_held, v_held], "expert", swap_mask[0])

    pre = rows_times_rows(taken[:units2], tokens)
    added = jax.nn.silu(pre[:units]) * pre[units:] * route_prob
    target = dest_slot[0]
    earlier = jnp.arange(rows)[:, None] < jnp.arange(rows)[None, :]
    same = target[:, None] == target[None, :]
    position = jnp.sum((same & earlier).astype(jnp.int32), 0)
    place = (target * capacity + position)[None]
    table = jnp.concatenate(
        [added, (dest_row + 1).astype(jnp.float32), place.astype(jnp.float32)], 0
    ).astype(jnp.bfloat16)
    side = jnp.concatenate([jnp.pad(taken[units2:], ((0, 2), (0, 0))), table], 1)
    side = lax.ppermute(side, "section", onward)

    factors = side[:units, width:]
    label = side[units, width:]
    place = side[units + 1, width:].astype(jnp.int32)
    total = arrived_base + columns_times_columns(factors, side[:units, :width])
    label = jnp.broadcast_to(label[:, None], (rows, LANES))
    payload = jnp.concatenate([total.astype(jnp.bfloat16), label], 1)
    pick = (jnp.arange(peers * capacity)[:, None] == place[None]).astype(jnp.bfloat16)
    packed = jnp.dot(pick, payload, preferred_element_type=jnp.float32).astype(jnp.bfloat16)
    packed = packed.reshape(peers, capacity, width + LANES)
    got = lax.all_to_all(packed, "expert", split_axis=0, concat_axis=0, tiled=True)
    got = got.reshape(peers * capacity, width + LANES)
    labels = got[:, width].astype(jnp.int32)
    put = (jnp.arange(1, out_rows + 1)[:, None] == labels[None]).astype(jnp.bfloat16)
    routed = jnp.dot(put, got[:, :width], preferred_element_type=jnp.float32)
    return (routed.astype(jnp.bfloat16)[None], m_recv[None], v_recv[None])


def solution(mesh):
    spec2, spec3 = P("expert", "section"), P("expert", "section", None)
    spec4 = P("expert", "section", None, None)
    in_specs = (spec3, spec2, spec4, spec4, spec3, spec3, spec2, P("section"), spec2, spec2)
    return jax.shard_map(
        per_device, mesh=mesh, in_specs=in_specs, out_specs=(spec3,) * 3, check_vma=False
    )
```

time: 113 us -> 60.2 us (0.53)
  local copies, waits for them, and re-layouts: 49.5 us -> 2 us
  waiting for transfers between devices: 27 us -> 35 us
  blocking collectives: 7.22 us -> 0 us
  other arithmetic: 4.77 us -> 0.3 us
  starting transfers between devices: 17.1 us -> 12.7 us
  matrix products: 3.5 us -> 7.19 us
    scatter x3 -> x0, local copies, waits for them, and re-layouts: 38 us -> none  [the longest x1 27.8 us: pack_rows(): packed = jnp.zeros((peer_count, capacity, model_width), jnp.bfloat16).at[...]
    all_to_all x1 -> x0, blocking collectives: 7.22 us -> none  [per_device(): lax.all_to_all(labels, 'expert', split_axis=0, concat_axis=0, tiled=True)]
    ppermute x9 -> x5, waiting for transfers between devices: 7.03 us -> 13.3 us  [the longest x3 9.17 us: exchange(): lax.ppermute(x, axis, r)]
    ppermute x9 -> x5, starting transfers between devices: 13.5 us -> 9 us  [the longest x3 3.58 us: exchange(): lax.ppermute(x, axis, r)]
    dot_general x2 -> x6, matrix products: 3.5 us -> 7.19 us  [the longest x2 2.08 us: rows_times_rows(): lax.dot_general(a, b, (((1,), (1,)), ((), ())), preferred_element_type=jn...]
    squeeze x3 -> x2, local copies, waits for them, and re-layouts: 3.12 us -> 0.03 us  [the longest x1 0.02 us: per_device(): given_down = lax.dynamic_index_in_dim(w_down[0], panel, 0, keepdims=False)]
    reshape x3 -> x0, local copies, waits for them, and re-layouts: 2.72 us -> none  [the longest x1 1.58 us: per_device(): gate_w = new_in[:, :unit_count].reshape(panels * unit_count, model_width)]
    broadcast_in_dim x6 -> x1, local copies, waits for them, and re-layouts: 2.78 us -> 0.08 us  [per_device(): label = jnp.broadcast_to(label[:, None], (rows, LANES))]
  transfers between devices with their start and end apart: 10 -> 6, of which waited for: 4 -> 3; matrix products, arithmetic and copies ran while one was open for 47% -> 1% of each run, Pallas kernels for 0% -> 0%
where the time goes in v1:
time: 60.2 us; the launch traced here: 59.5 us
  waiting for transfers between devices  35 us (58%)
  starting transfers between devices  12.7 us (21%)
  matrix products  7.19 us (12%)
  between operations  2.21 us (4%)
  local copies, waits for them, and re-layouts  2 us (3%)
    all_to_all x1, waiting for transfers between devices, per_device(): lax.all_to_all(packed, 'expert', split_axis=0, concat_axis=0, tiled=True)  21.7 us
    ppermute x3, waiting for transfers between devices, exchange(): lax.ppermute(x, axis, r)  9.17 us
    ppermute x1, waiting for transfers between devices, per_device(): side = lax.ppermute(side, 'section', onward)  4.09 us
    all_to_all x1, starting transfers between devices, per_device(): lax.all_to_all(packed, 'expert', split_axis=0, concat_axis=0, tiled=True)  3.73 us
    ppermute x3, starting transfers between devices, exchange(): lax.ppermute(x, axis, r)  3.58 us
    ppermute x1, starting transfers between devices, per_device(): arrived_base = lax.ppermute(base, 'section', onward)  3.03 us
    ppermute x1, starting transfers between devices, per_device(): side = lax.ppermute(side, 'section', onward)  2.4 us
    dot_general x2, matrix products, rows_times_rows(): lax.dot_general(a, b, (((1,), (1,)), ((), ())), preferred_element_type=jn...  2.08 us
  transfers between devices with their start and end apart: 6, of which 3 were waited for; matrix products, arithmetic and copies ran while one was open for 1% of the time, Pallas kernels for 0%

profile of v1, /device:TPU:0, one launch (start us, length us, event | category | flops | bytes accessed | tf_op | source)
XLA Modules:
  0.0 59.5 jit_solution(9622794323125215644)
XLA Ops:
  0.6 0.0 copy-start
  0.6 0.0 copy-start.6
  0.7 0.0 copy-start.3
  0.7 0.0 copy-start.2
  0.7 0.0 copy-start.9
  0.7 1.4 %copy-done = bf16[1,32,8,3072]{3,2,1,0:T(8,128)(2,1)S(1)} copy-done((bf16[1,32,8,3072]{3,2,1,0:T(8,128)(2,1)S(1)}, bf16[1,32,8,3072]{3,2,1,0:T(8,128)(2,1)}, u32[]{:S(2)}) %copy-start) | copy-done | bytes 1572888
  2.0 1.8 %fusion.4 = f32[128,256]{1,0:T(8,128)S(1)} fusion(bf16[1,32,8,3072]{3,2,1,0:T(8,128)(2,1)S(1)} %copy-done, bf16[1,128,3072]{2,1,0:T(8,128)(2,1)} %param.18), kind=kOutput, calls=%fused_computation.7 | convolution fusion | flops 201326592 | bytes 2490368 | tf_op jit(solution)/shard_map/dot_general | solution.py:23
  3.8 0.1 slice.50
  4.6 0.0 copy-done.6
  4.7 0.0 copy-done.3
  4.7 0.0 copy-done.2
  4.7 0.1 copy_bitcast_fusion
  4.8 0.0 copy-done.9
  4.8 1.4 %fusion = bf16[128,3072]{1,0:T(8,128)(2,1)} fusion(bf16[32,4,3072]{2,1,0:T(4,128)(2,1)S(1)} %bitcast.80, f32[128]{0:T(128)S(1)} %bitcast.82, f32[128,4]{1,0:T(8,128)S(1)} %slice.51, f32[128,252]{1,0:T(8,128)S(1)} %slice.50, f32[128,256]{1,0:T(8,128)S(1)} %fusion.4, pred[256]{0:T(512)(128)(4,1)S(1)} %compare_and_fusion), kind=kOutput, calls=%fused_computation.3 | convolution fusion | flops 202375168 | bytes 1835776 | tf_op jit(solution)/shard_map/dot_general | solution.py:50
  6.2 3.0 %collective-permute-start.22 = (bf16[128,3072]{1,0:T(8,128)(2,1)}, bf16[128,3072]{1,0:T(8,128)(2,1)S(1)}, u32[]{:S(2)}, u32[]{:S(2)}) collective-permute-start(bf16[128,3072]{1,0:T(8,128)(2,1)} %fusion), channel_id=1, source_target_pairs={{0,1},{1,2},{2,3},{3,0},{4,5},{5,6},{6,7},{7,4},{8,9},{9,10},{10,1... | collective-permute-start | bytes 2359304 | tf_op jit(solution)/shard_map/ppermute | solution.py:57
  9.8 0.0 copy-start.1
  9.8 0.0 copy-start.7
  9.9 0.0 copy-start.8
  9.9 13.1 %conditional.1 = (bf16[12,3072]{1,0:T(8,128)(2,1)S(1)}, f32[1,12,3072]{2,0,1:T(1,128)S(1)}, f32[1,12,3072]{2,0,1:T(1,128)S(1)}) conditional(s32[]{:T(128)} %bitcast.16, (bf16[12,3072]{1,0:T(8,128)(2,1)S(1)}, f32[12,3072]{1,0:T(8,128)S(1)}, f32[12,3072]{1,0:T(8,128)S(1)}) %tuple.91, (bf16[12,3072]{1,0:T(8,128)(2,1)S(1)}, ...), branch_computations={%region_0.1_spmd, %region_1.2_spmd, %region_2.3_spmd, %region_3.4_... | conditional | bytes 2211984 | solution.py:17
  9.9 1.6 %collective-permute-start.4 = (f32[12,3072]{1,0:T(8,128)S(1)}, f32[12,3072]{1,0:T(8,128)S(1)}, u32[]{:S(2)}, u32[]{:S(2)}) collective-permute-start(f32[12,3072]{1,0:T(8,128)S(1)} %get-tuple-element.68), channel_id=1, source_target_pairs={{0,8},{4,12},{8,0},{12,4},{16,24},{20,28},{24,16},{28,20},{1,9},{5... | collective-permute-start | bytes 442376 | tf_op jit(solution)/shard_map/cond/branch_2_fun/ppermute | solution.py:16
  11.5 0.5 collective-permute-start.5
  12.0 1.5 %collective-permute-start.3 = (bf16[12,3072]{1,0:T(8,128)(2,1)S(1)}, bf16[12,3072]{1,0:T(8,128)(2,1)S(1)}, u32[]{:S(2)}, u32[]{:S(2)}) collective-permute-start(bf16[12,3072]{1,0:T(8,128)(2,1)S(1)} %get-tuple-element.67), channel_id=1, source_target_pairs={{0,8},{4,12},{8,0},{12,4},{16,24},{20,28},{24,16},{28,20},{1,9},{5... | collective-permute-start | bytes 221192 | tf_op jit(solution)/shard_map/cond/branch_2_fun/ppermute | solution.py:16
  13.5 9.2 %collective-permute-done.3 = bf16[12,3072]{1,0:T(8,128)(2,1)S(1)} collective-permute-done((bf16[12,3072]{1,0:T(8,128)(2,1)S(1)}, bf16[12,3072]{1,0:T(8,128)(2,1)S(1)}, u32[]{:S(2)}, u32[]{:S(2)}) %collective-permute-start.3) | collective-permute-done | bytes 73760 | tf_op jit(solution)/shard_map/cond/branch_2_fun/ppermute | solution.py:16
  22.7 0.0 collective-permute-done.4
  22.7 0.2 copy.24
  22.8 0.0 collective-permute-done.5
  22.8 0.2 copy.32
  23.0 0.0 copy-start.4
  23.0 0.0 copy-start.5
  23.0 0.0 copy-done.1
  23.0 0.3 fusion.10
  23.4 0.0 copy-done.7
  23.4 0.1 convert_reduce_fusion.1
  23.5 0.0 copy-done.8
  23.6 2.4 %collective-permute-start.21 = (bf16[6,3200]{1,0:T(8,128)(2,1)S(1)}, bf16[6,3200]{1,0:T(8,128)(2,1)S(1)}, u32[]{:S(2)}, u32[]{:S(2)}) collective-permute-start(bf16[6,3200]{1,0:T(8,128)(2,1)S(1)} %fusion.25), channel_id=1, source_target_pairs={{0,1},{1,2},{2,3},{3,0},{4,5},{5,6},{6,7},{7,4},{8,9},{9,10},{10,1... | collective-permute-start | bytes 115208 | tf_op jit(solution)/shard_map/ppermute | solution.py:71
  26.0 4.1 %collective-permute-done.21 = bf16[6,3200]{1,0:T(8,128)(2,1)S(1)} collective-permute-done((bf16[6,3200]{1,0:T(8,128)(2,1)S(1)}, bf16[6,3200]{1,0:T(8,128)(2,1)S(1)}, u32[]{:S(2)}, u32[]{:S(2)}) %collective-permute-start.21) | collective-permute-done | bytes 38432 | tf_op jit(solution)/shard_map/ppermute | solution.py:71
  30.1 0.0 copy-done.4
  30.1 0.0 copy-done.5
  30.1 0.0 collective-permute-done.22
  30.1 0.4 add_convert_fusion
  30.5 0.1 broadcast_in_dim.75
  30.6 1.8 %convolution_convert_fusion = bf16[256,3200]{1,0:T(8,128)(2,1)} fusion(bf16[128,128]{1,0:T(8,128)(2,1)S(1)} %broadcast_in_dim.75, bf16[128,3072]{1,0:T(8,128)(2,1)S(1)} %add_convert_fusion, s32[128]{0:T(128)S(1)} %get-tuple-element.121), kind=kOutput, calls=%fused_computation | convolution fusion | flops 212205568 | bytes 2458112 | tf_op jit(solution)/shard_map/dot_general | solution.py:80
  32.4 3.7 %all-to-all-start = ((bf16[8,32,3200]{2,1,0:T(8,128)(2,1)}), bf16[8,32,3200]{2,1,0:T(8,128)(2,1)S(1)}, u32[]{:S(2)}, u32[]{:S(2)}) async-start(bf16[8,32,3200]{2,1,0:T(8,128)(2,1)} %bitcast.63), calls=%async_computation | async-start | bytes 3276800 | tf_op jit(solution)/shard_map/all_to_all | solution.py:82
  36.1 21.7 %all-to-all-done = bf16[8,32,3200]{2,1,0:T(8,128)(2,1)S(1)} async-done(((bf16[8,32,3200]{2,1,0:T(8,128)(2,1)}), bf16[8,32,3200]{2,1,0:T(8,128)(2,1)S(1)}, u32[]{:S(2)}, u32[]{:S(2)}) %all-to-all-start) | async-done | bytes 1638432 | tf_op jit(solution)/shard_map/all_to_all | solution.py:82
  57.9 0.1 convert_reduce_fusion
  58.0 1.5 %fusion.1 = bf16[1,192,3072]{2,1,0:T(8,128)(2,1)} fusion(bf16[256,3200]{1,0:T(8,128)(2,1)S(1)} %bitcast.62, s32[256]{0:T(256)S(1)} %convert_reduce_fusion, s32[192]{0:T(256)S(1)} %iota_add_fusion), kind=kOutput, calls=%fused_computation.4 | convolution fusion | flops 302628864 | bytes 2754560 | tf_op jit(solution)/shard_map/dot_general | solution.py:86
  (12 shorter events, 0.1 us)
Async XLA Ops:
  0.6 1.4 %copy-start = (bf16[1,32,8,3072]{3,2,1,0:T(8,128)(2,1)S(1)}, bf16[1,32,8,3072]{3,2,1,0:T(8,128)(2,1)}, u32[]{:S(2)}) copy-start(bf16[1,32,8,3072]{3,2,1,0:T(8,128)(2,1)} %param.20) | copy-start | bytes 4718596
  0.6 4.0 %copy-start.6 = (bf16[1,32,4,3072]{3,2,1,0:T(4,128)(2,1)S(1)}, bf16[1,32,4,3072]{3,2,1,0:T(4,128)(2,1)}, u32[]{:S(2)}) copy-start(bf16[1,32,4,3072]{3,2,1,0:T(4,128)(2,1)} %param.21) | copy-start | bytes 2359300
  0.7 4.0 %copy-start.3 = (f32[1,12,3072]{2,0,1:T(1,128)S(1)}, f32[1,12,3072]{2,0,1:T(1,128)}, u32[]{:S(2)}) copy-start(f32[1,12,3072]{2,0,1:T(1,128)} %param.22) | copy-start | bytes 442372
  0.7 4.0 %copy-start.2 = (f32[1,12,3072]{2,0,1:T(1,128)S(1)}, f32[1,12,3072]{2,0,1:T(1,128)}, u32[]{:S(2)}) copy-start(f32[1,12,3072]{2,0,1:T(1,128)} %param.23) | copy-start | bytes 442372
  0.7 4.1 %copy-start.9 = (f32[1,128]{1,0:T(1,128)S(1)}, f32[1,128]{1,0:T(1,128)}, u32[]{:S(2)}) copy-start(f32[1,128]{1,0:T(1,128)} %param.19) | copy-start | bytes 1540
  6.2 23.9 %collective-permute-start.22 = (bf16[128,3072]{1,0:T(8,128)(2,1)}, bf16[128,3072]{1,0:T(8,128)(2,1)S(1)}, u32[]{:S(2)}, u32[]{:S(2)}) collective-permute-start(bf16[128,3072]{1,0:T(8,128)(2,1)} %fusion), channel_id=1, source_target_pairs={{0,1},{1,2},{2,3},{3,0},{4,5},{5,6},{6,7},{7,4},{8,9},{9,10},{10,1... | collective-permute-start | bytes 2359304 | tf_op jit(solution)/shard_map/ppermute | solution.py:57
  9.8 13.2 %copy-start.1 = (bf16[1,128,3072]{2,1,0:T(8,128)(2,1)S(1)}, bf16[1,128,3072]{2,1,0:T(8,128)(2,1)}, u32[]{:S(2)}) copy-start(bf16[1,128,3072]{2,1,0:T(8,128)(2,1)} %param.18) | copy-start | bytes 2359300
  9.8 13.5 %copy-start.7 = (s32[1,128]{1,0:T(1,128)S(1)}, s32[1,128]{1,0:T(1,128)}, u32[]{:S(2)}) copy-start(s32[1,128]{1,0:T(1,128)} %param.26) | copy-start | bytes 1540
  9.9 13.6 %copy-start.8 = (s32[1,128]{1,0:T(1,128)S(1)}, s32[1,128]{1,0:T(1,128)}, u32[]{:S(2)}) copy-start(s32[1,128]{1,0:T(1,128)} %param.27) | copy-start | bytes 1540
  9.9 12.8 %collective-permute-start.4 = (f32[12,3072]{1,0:T(8,128)S(1)}, f32[12,3072]{1,0:T(8,128)S(1)}, u32[]{:S(2)}, u32[]{:S(2)}) collective-permute-start(f32[12,3072]{1,0:T(8,128)S(1)} %get-tuple-element.68), channel_id=1, source_target_pairs={{0,8},{4,12},{8,0},{12,4},{16,24},{20,28},{24,16},{28,20},{1,9},{5... | collective-permute-start | bytes 442376 | tf_op jit(solution)/shard_map/cond/branch_2_fun/ppermute | solution.py:16
  11.5 11.4 %collective-permute-start.5 = (f32[12,3072]{1,0:T(8,128)S(1)}, f32[12,3072]{1,0:T(8,128)S(1)}, u32[]{:S(2)}, u32[]{:S(2)}) collective-permute-start(f32[12,3072]{1,0:T(8,128)S(1)} %get-tuple-element.69), channel_id=1, source_target_pairs={{0,8},{4,12},{8,0},{12,4},{16,24},{20,28},{24,16},{28,20},{1,9},{5... | collective-permute-start | bytes 442376 | tf_op jit(solution)/shard_map/cond/branch_2_fun/ppermute | solution.py:16
  12.0 10.7 %collective-permute-start.3 = (bf16[12,3072]{1,0:T(8,128)(2,1)S(1)}, bf16[12,3072]{1,0:T(8,128)(2,1)S(1)}, u32[]{:S(2)}, u32[]{:S(2)}) collective-permute-start(bf16[12,3072]{1,0:T(8,128)(2,1)S(1)} %get-tuple-element.67), channel_id=1, source_target_pairs={{0,8},{4,12},{8,0},{12,4},{16,24},{20,28},{24,16},{28,20},{1,9},{5... | collective-permute-start | bytes 221192 | tf_op jit(solution)/shard_map/cond/branch_2_fun/ppermute | solution.py:16
  23.0 7.0 %copy-start.4 = (f32[1,12,3072]{2,0,1:T(1,128)}, f32[1,12,3072]{2,0,1:T(1,128)S(1)}, u32[]{:S(2)}) copy-start(f32[1,12,3072]{2,0,1:T(1,128)S(1)} %get-tuple-element.119) | copy-start | bytes 442372
  23.0 7.0 %copy-start.5 = (f32[1,12,3072]{2,0,1:T(1,128)}, f32[1,12,3072]{2,0,1:T(1,128)S(1)}, u32[]{:S(2)}) copy-start(f32[1,12,3072]{2,0,1:T(1,128)S(1)} %get-tuple-element.120) | copy-start | bytes 442372
  23.6 6.5 %collective-permute-start.21 = (bf16[6,3200]{1,0:T(8,128)(2,1)S(1)}, bf16[6,3200]{1,0:T(8,128)(2,1)S(1)}, u32[]{:S(2)}, u32[]{:S(2)}) collective-permute-start(bf16[6,3200]{1,0:T(8,128)(2,1)S(1)} %fusion.25), channel_id=1, source_target_pairs={{0,1},{1,2},{2,3},{3,0},{4,5},{5,6},{6,7},{7,4},{8,9},{9,10},{10,1... | collective-permute-start | bytes 115208 | tf_op jit(solution)/shard_map/ppermute | solution.py:71
  32.4 25.5 %all-to-all-start = ((bf16[8,32,3200]{2,1,0:T(8,128)(2,1)}), bf16[8,32,3200]{2,1,0:T(8,128)(2,1)S(1)}, u32[]{:S(2)}, u32[]{:S(2)}) async-start(bf16[8,32,3200]{2,1,0:T(8,128)(2,1)} %bitcast.63), calls=%async_computation | async-start | bytes 3276800 | tf_op jit(solution)/shard_map/all_to_all | solution.py:82

commit v2 on v1

v2 whole, which is shorter than its diff:
```python
import jax
import jax.numpy as jnp
from jax import lax
from jax.sharding import PartitionSpec as P

LANES = 128


FIRST, SECOND = 5, 3


def exchange(pair_mask, axis, held, program):
    size = lax.axis_size(axis)
    low = 0
    while True:
        bits = min(3, size.bit_length() - 1 - low)
        last = (1 << (low + bits)) == size
        digit = jnp.bitwise_and(jnp.right_shift(pair_mask, low), (1 << bits) - 1)

        def arm(k, low=low, last=last):
            route = [(i, i ^ (k << low)) for i in range(size)]
            swap = (lambda x: lax.ppermute(x, axis, route)) if k else (lambda x: x)
            return lambda h: program(swap, h) if last else [swap(x) for x in h]

        least = 1 if last and low == 0 else 0
        held = lax.switch(digit - least, [arm(k) for k in range(least, 1 << bits)], held)
        if last:
            return held
        low += bits


def rows_times_rows(a, b):
    return lax.dot_general(a, b, (((1,), (1,)), ((), ())), preferred_element_type=jnp.float32)


def per_device(
    rows_in, route_prob, w_in, w_down, m_send, v_send, chosen, swap_mask, dest_slot, dest_row
):
    panels, units2, width = w_in.shape[1:]
    units = units2 // 2
    peers = lax.axis_size("expert")
    sections = lax.axis_size("section")
    tokens = rows_in[0]
    rows = tokens.shape[0]
    capacity = 2 * rows // peers
    out_rows = rows + rows // 2
    panel = chosen[0, 0]
    onward = [(i, (i + 1) % sections) for i in range(sections)]
    edge = width * FIRST // (FIRST + SECOND)

    def next_section(x):
        return lax.ppermute(x, "section", onward)

    def pick_rows(place, x):
        pick = (jnp.arange(peers * capacity)[:, None] == place[None]).astype(jnp.bfloat16)
        return jnp.dot(pick, x, preferred_element_type=jnp.float32).astype(jnp.bfloat16)

    def put_rows(labels, x):
        put = (jnp.arange(1, out_rows + 1)[:, None] == labels[None]).astype(jnp.bfloat16)
        return jnp.dot(put, x, preferred_element_type=jnp.float32).astype(jnp.bfloat16)

    def deal(packed):
        packed = packed.reshape(peers, capacity, packed.shape[1])
        got = lax.all_to_all(packed, "expert", split_axis=0, concat_axis=0, tiled=True)
        return got.reshape(peers * capacity, got.shape[2])

    def program(swap, held):
        given, m_held, v_held = held
        taken = swap(given)

        pre = rows_times_rows(tokens, w_in[0].reshape(panels * units2, width))
        column = jnp.arange(panels * units2)
        stays = (column % units2 < units) & (column // units2 != panel)
        hidden = jax.nn.silu(pre) * jnp.roll(pre, -units, 1)
        hidden = jnp.where(stays[None], hidden, 0).astype(jnp.bfloat16)
        down = jnp.pad(w_down[0], ((0, 0), (0, units), (0, 0))).reshape(panels * units2, width)
        mixed = jnp.dot(hidden, down, preferred_element_type=jnp.float32)
        taken, mixed = lax.optimization_barrier((taken, mixed))

        pre = rows_times_rows(tokens, taken[:units2])
        hidden = (jax.nn.silu(pre[:, :units]) * pre[:, units:]).astype(jnp.bfloat16)
        mixed = mixed + jnp.dot(hidden, taken[units2:], preferred_element_type=jnp.float32)
        base = (route_prob[0][:, None] * mixed).astype(jnp.bfloat16)

        target = dest_slot[0]
        earlier = jnp.arange(rows)[:, None] < jnp.arange(rows)[None, :]
        same = target[:, None] == target[None, :]
        position = jnp.sum((same & earlier).astype(jnp.int32), 0)
        place = target * capacity + position
        label = jnp.broadcast_to((dest_row[0] + 1).astype(jnp.bfloat16)[:, None], (rows, LANES))

        first, second = base[:, :edge], base[:, edge:]
        m_recv, v_recv = swap(m_held), swap(v_held)
        first, second, places = lax.optimization_barrier((first, second, place))
        first = next_section(first)
        places = next_section(places)
        second, m_recv, v_recv = lax.optimization_barrier((second, m_recv, v_recv))
        second = deal(pick_rows(place, jnp.concatenate([second, label], 1)))
        labels = second[:, width - edge].astype(jnp.int32)
        second = next_section(put_rows(labels, second[:, : width - edge]))
        labels = next_section(labels)
        first = put_rows(labels, deal(pick_rows(places, first)))
        return jnp.concatenate([first, second], 1)[None], m_recv.swapaxes(0, 1), v_recv.swapaxes(0, 1)

    given_in = lax.dynamic_index_in_dim(w_in[0], panel, 0, keepdims=False)
    given_down = lax.dynamic_index_in_dim(w_down[0], panel, 0, keepdims=False)
    given = jnp.concatenate([given_in, given_down], 0)
    return tuple(exchange(swap_mask[0], "expert", [given, m_send.swapaxes(0, 1), v_send.swapaxes(0, 1)], program))


def solution(mesh):
    spec2, spec3 = P("expert", "section"), P("expert", "section", None)
    spec4 = P("expert", "section", None, None)
    in_specs = (spec3, spec2, spec4, spec4, spec3, spec3, spec2, P("section"), spec2, spec2)
    return jax.shard_map(
        per_device, mesh=mesh, in_specs=in_specs, out_specs=(spec3,) * 3, check_vma=False
    )
```

time: 60.2 us -> 56.5 us (0.939)
  waiting for transfers between devices: 35 us -> 23.5 us
  local copies, waits for them, and re-layouts: 2 us -> 5.4 us
  starting transfers between devices: 12.7 us -> 15.3 us
  other arithmetic: 0.3 us -> 2.43 us
  loops' own time: 0.07 us -> 0.68 us
    all_to_all x1 -> x2, waiting for transfers between devices: 21.7 us -> 1.89 us  [deal(): lax.all_to_all(packed, 'expert', split_axis=0, concat_axis=0, tiled=True)]
    ppermute x5 -> x7, waiting for transfers between devices: 13.3 us -> 21.6 us  [the longest x4 19.3 us: next_section(): return lax.ppermute(x, 'section', onward)]
    all_to_all x1 -> x2, starting transfers between devices: 3.73 us -> 7.31 us  [deal(): lax.all_to_all(packed, 'expert', split_axis=0, concat_axis=0, tiled=True)]
    another operation x0 -> x2, local copies, waits for them, and re-layouts: none -> 1.96 us
    unnamed x21 -> x0, local copies, waits for them, and re-layouts: 1.47 us -> none
    cond x3 -> x12, local copies, waits for them, and re-layouts: 0.31 us -> 1.65 us  [the longest x2 1.63 us: exchange(): lax.switch(digit - least, [arm(k) for k in range(least, 1 << bits)], held)]
    broadcast_in_dim x0 -> x1, other arithmetic: none -> 1.16 us  [program(): jnp.concatenate([first, second], 1)[None]]
    ppermute x5 -> x7, starting transfers between devices: 9 us -> 7.97 us  [the longest x3 6.15 us: arm(): swap = (lambda x: lax.ppermute(x, axis, route)) if k else lambda x: x]
  transfers between devices with their start and end apart: 6 -> 9, of which waited for: 3 -> 4; matrix products, arithmetic and copies ran while one was open for 1% -> 21% of each run, Pallas kernels for 0% -> 0%
where the time goes in v2:
time: 56.5 us; the launch traced here: 56.1 us
  waiting for transfers between devices  23.5 us (42%)
  starting transfers between devices  15.3 us (27%)
  matrix products  6.78 us (12%)
  local copies, waits for them, and re-layouts  5.4 us (10%)
  other arithmetic  2.43 us (4%)
  between operations  1.94 us (3%)
  loops' own time  0.68 us (1%)
    ppermute x4, waiting for transfers between devices, next_section(): return lax.ppermute(x, 'section', onward)  19.3 us
    all_to_all x2, starting transfers between devices, deal(): lax.all_to_all(packed, 'expert', split_axis=0, concat_axis=0, tiled=True)  7.31 us
    ppermute x3, starting transfers between devices, arm(): swap = (lambda x: lax.ppermute(x, axis, route)) if k else lambda x: x  6.15 us
    dot_general x2, matrix products, rows_times_rows(): lax.dot_general(a, b, (((1,), (1,)), ((), ())), preferred_element_type=jn...  2.61 us
    dot_general x2, matrix products, pick_rows(): jnp.dot(pick, x, preferred_element_type=jnp.float32).astype(jnp.bfloat16)  2.53 us
    ppermute x3, waiting for transfers between devices, arm(): swap = (lambda x: lax.ppermute(x, axis, route)) if k else lambda x: x  2.38 us
    another operation x2, local copies, waits for them, and re-layouts  1.96 us
    all_to_all x2, waiting for transfers between devices, deal(): lax.all_to_all(packed, 'expert', split_axis=0, concat_axis=0, tiled=True)  1.89 us
  transfers between devices with their start and end apart: 9, of which 4 were waited for; matrix products, arithmetic and copies ran while one was open for 21% of the time, Pallas kernels for 0%

profile of v2, /device:TPU:0, one launch (start us, length us, event | category | flops | bytes accessed | tf_op | source)
XLA Modules:
  0.0 56.1 jit_solution(17598357011401894614)
XLA Ops:
  1.3 0.8 %dynamic-slice_bitcast_fusion = bf16[8,3072]{1,0:T(8,128)(2,1)S(1)} fusion(bf16[1,32,8,3072]{3,2,1,0:T(8,128)(2,1)} %param.19, s32[]{:T(128)S(6)} %select_n.138), kind=kLoop, calls=%fused_computation.442 | loop fusion | bytes 98308 | tf_op jit(solution)/shard_map/jit(dynamic_index_in_dim)/squeeze | solution.py:105
  2.1 0.7 %dynamic-slice_bitcast_fusion.1 = bf16[4,3072]{1,0:T(4,128)(2,1)S(1)} fusion(bf16[1,32,4,3072]{3,2,1,0:T(4,128)(2,1)} %param.20, s32[]{:T(128)S(6)} %select_n.138), kind=kLoop, calls=%fused_computation.443 | loop fusion | bytes 49156 | tf_op jit(solution)/shard_map/jit(dynamic_index_in_dim)/squeeze | solution.py:106
  3.5 52.5 %conditional.1 = (bf16[1,192,3072]{2,1,0:T(8,128)(2,1)}, f32[1,12,3072]{2,0,1:T(1,128)}, f32[1,12,3072]{2,0,1:T(1,128)}) conditional(s32[]{:T(128)} %bitcast.133, (s32[1,128]{1,0:T(1,128)}, f32[1,128]{1,0:T(1,128)}, bf16[12,3072]{1,0:T(8,128)(2,1)S(1)}, s32[]{:T(128)}, bf16[1,32,8,3072]{3,2,1,0:T(8,128)(2,1)}, ...), branch_computations={%region_0.2_spmd, %region_2.4_spmd, %region_4.6_spmd, %region_6.8_... | conditional | flops 929914688 | bytes 38544896 | solution.py:26
  4.0 3.4 %collective-permute-start.42 = (bf16[12,3072]{1,0:T(8,128)(2,1)S(1)}, bf16[12,3072]{1,0:T(8,128)(2,1)S(1)}, u32[]{:S(2)}, u32[]{:S(2)}) collective-permute-start(bf16[12,3072]{1,0:T(8,128)(2,1)S(1)} %get-tuple-element.250), channel_id=1, source_target_pairs={{0,28},{4,24},{8,20},{12,16},{16,12},{20,8},{24,4},{28,0},{1,29},{... | collective-permute-start | bytes 221192 | tf_op jit(solution)/shard_map/cond/branch_6_fun/ppermute | solution.py:22
  7.4 0.9 %copy.188 = f32[1,12,3072]{2,1,0:T(8,128)S(1)} copy(f32[1,12,3072]{2,0,1:T(1,128)} %get-tuple-element.663) | data formatting | bytes 294912 | tf_op jit(solution)/shard_map
  8.3 0.1 collective-permute-start.43
  8.4 0.0 copy-start.34
  8.4 0.0 copy-start.13
  8.4 1.0 %copy.187 = f32[1,12,3072]{2,1,0:T(8,128)S(1)} copy(f32[1,12,3072]{2,0,1:T(1,128)} %get-tuple-element.664) | data formatting | bytes 294912 | tf_op jit(solution)/shard_map
  9.4 2.7 %collective-permute-start.44 = (f32[12,1,3072]{2,0,1:T(8,128)S(1)}, f32[12,1,3072]{2,0,1:T(8,128)S(1)}, u32[]{:S(2)}, u32[]{:S(2)}) collective-permute-start(f32[12,1,3072]{2,0,1:T(8,128)S(1)} %bitcast.351), channel_id=1, source_target_pairs={{0,28},{4,24},{8,20},{12,16},{16,12},{20,8},{24,4},{28,0},{1,29},{... | collective-permute-start | bytes 442376 | tf_op jit(solution)/shard_map/cond/branch_6_fun/ppermute | solution.py:22
  12.1 2.3 %fusion.242 = f32[128,256]{1,0:T(8,128)S(1)} fusion(bf16[1,32,8,3072]{3,2,1,0:T(8,128)(2,1)} %get-tuple-element.253, bf16[1,128,3072]{2,1,0:T(8,128)(2,1)} %get-tuple-element.362), kind=kOutput, calls=%fused_computation.384 | convolution fusion | flops 201326592 | bytes 2490368 | tf_op jit(solution)/shard_map/cond/branch_6_fun/dot_general | solution.py:33
  14.4 0.0 copy-start.6
  14.4 0.1 slice.248
  14.5 0.7 %compare_and_fusion.6 = pred[256]{0:T(512)(128)(4,1)S(1)} fusion(s32[]{:T(128)} %get-tuple-element.251), kind=kLoop, calls=%fused_computation.424 | loop fusion | flops 3840 | bytes 260 | tf_op jit(solution)/shard_map/cond/branch_6_fun/and | solution.py:73
  15.3 0.0 copy-done.27
  15.3 0.1 convert_reduce_fusion.13
  15.4 0.0 copy-done.34
  15.4 0.0 copy-done.13
  15.4 0.5 fusion.240
  15.9 0.0 copy-start.20
  15.9 0.0 collective-permute-done.42
  15.9 0.0 copy-done.6
  15.9 0.3 convolution_bitcast_fusion.6
  16.2 0.5 fusion.267
  16.7 0.3 multiply_convert_fusion.6
  17.1 0.4 collective-permute-start.47
  17.5 0.0 collective-permute-done.43
  17.5 2.4 %collective-permute-done.44 = f32[12,1,3072]{2,0,1:T(8,128)S(1)} collective-permute-done((f32[12,1,3072]{2,0,1:T(8,128)S(1)}, f32[12,1,3072]{2,0,1:T(8,128)S(1)}, u32[]{:S(2)}, u32[]{:S(2)}) %collective-permute-start.44) | collective-permute-done | bytes 147488 | tf_op jit(solution)/shard_map/cond/branch_6_fun/ppermute | solution.py:22
  19.8 0.1 broadcast_in_dim.150
  19.9 1.2 %convolution_convert_fusion.25 = bf16[256,1280]{1,0:T(8,128)(2,1)} fusion(bf16[128,128]{1,0:T(8,128)(2,1)S(1)} %broadcast_in_dim.150, bf16[128,1152]{1,0:T(8,128)(2,1)S(1)} %slice.251, s32[128]{0:T(128)S(1)} %get-tuple-element.683), kind=kOutput, calls=%fused_computation.379 | convolution fusion | flops 84901888 | bytes 983552 | tf_op jit(solution)/shard_map/cond/branch_6_fun/dot_general | solution.py:56
  21.1 3.8 %all-to-all-start.12 = ((bf16[8,32,1280]{2,1,0:T(8,128)(2,1)}), bf16[8,32,1280]{2,1,0:T(8,128)(2,1)S(1)}, u32[]{:S(2)}, u32[]{:S(2)}) async-start(bf16[8,32,1280]{2,1,0:T(8,128)(2,1)} %bitcast.126), calls=%async_computation.12 | async-start | bytes 1310720 | tf_op jit(solution)/shard_map/cond/branch_6_fun/all_to_all | solution.py:64
  24.9 0.0 collective-permute-start.46
  24.9 7.9 %collective-permute-done.46 = s32[128]{0:T(128)S(1)} collective-permute-done((s32[128]{0:T(128)S(1)}, s32[128]{0:T(128)S(1)}, u32[]{:S(2)}, u32[]{:S(2)}) %collective-permute-start.46) | collective-permute-done | bytes 544 | tf_op jit(solution)/shard_map/cond/branch_6_fun/ppermute | solution.py:52
  32.8 0.0 collective-permute-done.47
  32.8 1.4 %convolution_convert_fusion.24 = bf16[256,1920]{1,0:T(8,128)(2,1)} fusion(bf16[128,1920]{1,0:T(8,128)(2,1)S(1)} %collective-permute-done.47, s32[128]{0:T(128)S(1)} %collective-permute-done.46), kind=kOutput, calls=%fused_computation.378 | convolution fusion | flops 126353408 | bytes 1475072 | tf_op jit(solution)/shard_map/cond/branch_6_fun/dot_general | solution.py:56
  34.1 1.9 %all-to-all-done.12 = bf16[8,32,1280]{2,1,0:T(8,128)(2,1)S(1)} async-done(((bf16[8,32,1280]{2,1,0:T(8,128)(2,1)}), bf16[8,32,1280]{2,1,0:T(8,128)(2,1)S(1)}, u32[]{:S(2)}, u32[]{:S(2)}) %all-to-all-start.12) | async-done | bytes 655392 | tf_op jit(solution)/shard_map/cond/branch_6_fun/all_to_all | solution.py:64
  36.0 3.6 %all-to-all-start.13 = ((bf16[8,32,1920]{2,1,0:T(8,128)(2,1)}), bf16[8,32,1920]{2,1,0:T(8,128)(2,1)S(1)}, u32[]{:S(2)}, u32[]{:S(2)}) async-start(bf16[8,32,1920]{2,1,0:T(8,128)(2,1)} %bitcast.128), calls=%async_computation.13 | async-start | bytes 1966080 | tf_op jit(solution)/shard_map/cond/branch_6_fun/all_to_all | solution.py:64
  39.6 0.1 convert_reduce_fusion.12
  39.7 0.3 convolution_convert_fusion.26
  40.0 0.1 collective-permute-start.48
  40.1 1.4 %collective-permute-start.45 = (s32[256]{0:T(256)S(1)}, s32[256]{0:T(256)S(1)}, u32[]{:S(2)}, u32[]{:S(2)}) collective-permute-start(s32[256]{0:T(256)S(1)} %convert_reduce_fusion.12), channel_id=1, source_target_pairs={{0,1},{1,2},{2,3},{3,0},{4,5},{5,6},{6,7},{7,4},{8,9},{9,10},{10,1... | collective-permute-start | bytes 3080 | tf_op jit(solution)/shard_map/cond/branch_6_fun/ppermute | solution.py:52
  41.5 0.8 %copy.153 = f32[1,12,3072]{2,0,1:T(1,128)} copy(f32[1,12,3072]{2,1,0:T(8,128)S(1)} %bitcast.330) | data formatting | bytes 294912 | tf_op jit(solution)/shard_map/cond | solution.py:26
  42.3 0.8 %copy.160 = f32[1,12,3072]{2,0,1:T(1,128)} copy(f32[1,12,3072]{2,1,0:T(8,128)S(1)} %bitcast.337) | data formatting | bytes 294912 | tf_op jit(solution)/shard_map/cond | solution.py:26
  43.1 11.4 %collective-permute-done.45 = s32[256]{0:T(256)S(1)} collective-permute-done((s32[256]{0:T(256)S(1)}, s32[256]{0:T(256)S(1)}, u32[]{:S(2)}, u32[]{:S(2)}) %collective-permute-start.45) | collective-permute-done | bytes 1056 | tf_op jit(solution)/shard_map/cond/branch_6_fun/ppermute | solution.py:52
  54.5 0.0 all-to-all-done.13
  54.5 0.4 convolution_convert_fusion.27
  54.9 0.0 collective-permute-done.48
  54.9 1.2 %maximum_bitcast_fusion.6 = bf16[1,192,3072]{2,1,0:T(8,128)(2,1)} fusion(bf16[192,1152]{1,0:T(8,128)(2,1)S(1)} %collective-permute-done.48, bf16[192,1920]{1,0:T(8,128)(2,1)S(1)} %convolution_convert_fusion.27), kind=kLoop, calls=%fused_computation.388 | loop fusion | flops 2359296 | bytes 2359296 | tf_op jit(solution)/shard_map/cond/branch_6_fun/broadcast_in_dim | solution.py:103
  (9 shorter events, 0.1 us)
Async XLA Ops:
  4.0 11.9 %collective-permute-start.42 = (bf16[12,3072]{1,0:T(8,128)(2,1)S(1)}, bf16[12,3072]{1,0:T(8,128)(2,1)S(1)}, u32[]{:S(2)}, u32[]{:S(2)}) collective-permute-start(bf16[12,3072]{1,0:T(8,128)(2,1)S(1)} %get-tuple-element.250), channel_id=1, source_target_pairs={{0,28},{4,24},{8,20},{12,16},{16,12},{20,8},{24,4},{28,0},{1,29},{... | collective-permute-start | bytes 221192 | tf_op jit(solution)/shard_map/cond/branch_6_fun/ppermute | solution.py:22
  8.3 9.2 %collective-permute-start.43 = (f32[12,1,3072]{2,0,1:T(8,128)S(1)}, f32[12,1,3072]{2,0,1:T(8,128)S(1)}, u32[]{:S(2)}, u32[]{:S(2)}) collective-permute-start(f32[12,1,3072]{2,0,1:T(8,128)S(1)} %bitcast.344), channel_id=1, source_target_pairs={{0,28},{4,24},{8,20},{12,16},{16,12},{20,8},{24,4},{28,0},{1,29},{... | collective-permute-start | bytes 442376 | tf_op jit(solution)/shard_map/cond/branch_6_fun/ppermute | solution.py:22
  8.4 6.9 %copy-start.27 = (s32[1,128]{1,0:T(1,128)S(1)}, s32[1,128]{1,0:T(1,128)}, u32[]{:S(2)}) copy-start(s32[1,128]{1,0:T(1,128)} %get-tuple-element.320) | copy-start | bytes 1540 | tf_op jit(solution)/shard_map/cond
  8.4 7.0 %copy-start.34 = (s32[1,128]{1,0:T(1,128)S(1)}, s32[1,128]{1,0:T(1,128)}, u32[]{:S(2)}) copy-start(s32[1,128]{1,0:T(1,128)} %get-tuple-element.355) | copy-start | bytes 1540 | tf_op jit(solution)/shard_map/cond
  8.4 7.0 %copy-start.13 = (bf16[1,32,4,3072]{3,2,1,0:T(4,128)(2,1)S(1)}, bf16[1,32,4,3072]{3,2,1,0:T(4,128)(2,1)}, u32[]{:S(2)}) copy-start(bf16[1,32,4,3072]{3,2,1,0:T(4,128)(2,1)} %get-tuple-element.254) | copy-start | bytes 2359300 | tf_op jit(solution)/shard_map/cond
  9.4 10.4 %collective-permute-start.44 = (f32[12,1,3072]{2,0,1:T(8,128)S(1)}, f32[12,1,3072]{2,0,1:T(8,128)S(1)}, u32[]{:S(2)}, u32[]{:S(2)}) collective-permute-start(f32[12,1,3072]{2,0,1:T(8,128)S(1)} %bitcast.351), channel_id=1, source_target_pairs={{0,28},{4,24},{8,20},{12,16},{16,12},{20,8},{24,4},{28,0},{1,29},{... | collective-permute-start | bytes 442376 | tf_op jit(solution)/shard_map/cond/branch_6_fun/ppermute | solution.py:22
  14.4 1.5 %copy-start.6 = (bf16[1,128,3072]{2,1,0:T(8,128)(2,1)S(1)}, bf16[1,128,3072]{2,1,0:T(8,128)(2,1)}, u32[]{:S(2)}) copy-start(bf16[1,128,3072]{2,1,0:T(8,128)(2,1)} %get-tuple-element.362) | copy-start | bytes 2359300 | tf_op jit(solution)/shard_map/cond
  15.9 0.8 %copy-start.20 = (f32[1,128]{1,0:T(1,128)S(1)}, f32[1,128]{1,0:T(1,128)}, u32[]{:S(2)}) copy-start(f32[1,128]{1,0:T(1,128)} %get-tuple-element.327) | copy-start | bytes 1540 | tf_op jit(solution)/shard_map/cond
  17.1 15.7 %collective-permute-start.47 = (bf16[128,1920]{1,0:T(8,128)(2,1)S(1)}, bf16[128,1920]{1,0:T(8,128)(2,1)S(1)}, u32[]{:S(2)}, u32[]{:S(2)}) collective-permute-start(bf16[128,1920]{1,0:T(8,128)(2,1)S(1)} %slice.250), channel_id=1, source_target_pairs={{0,1},{1,2},{2,3},{3,0},{4,5},{5,6},{6,7},{7,4},{8,9},{9,10},{10,1... | collective-permute-start | bytes 1474568 | tf_op jit(solution)/shard_map/cond/branch_6_fun/ppermute | solution.py:52
  21.1 14.9 %all-to-all-start.12 = ((bf16[8,32,1280]{2,1,0:T(8,128)(2,1)}), bf16[8,32,1280]{2,1,0:T(8,128)(2,1)S(1)}, u32[]{:S(2)}, u32[]{:S(2)}) async-start(bf16[8,32,1280]{2,1,0:T(8,128)(2,1)} %bitcast.126), calls=%async_computation.12 | async-start | bytes 1310720 | tf_op jit(solution)/shard_map/cond/branch_6_fun/all_to_all | solution.py:64
  24.9 7.9 %collective-permute-start.46 = (s32[128]{0:T(128)S(1)}, s32[128]{0:T(128)S(1)}, u32[]{:S(2)}, u32[]{:S(2)}) collective-permute-start(s32[128]{0:T(128)S(1)} %multiply_add_fusion.6), channel_id=1, source_target_pairs={{0,1},{1,2},{2,3},{3,0},{4,5},{5,6},{6,7},{7,4},{8,9},{9,10},{10,1... | collective-permute-start | bytes 1544 | tf_op jit(solution)/shard_map/cond/branch_6_fun/ppermute | solution.py:52
  36.0 18.4 %all-to-all-start.13 = ((bf16[8,32,1920]{2,1,0:T(8,128)(2,1)}), bf16[8,32,1920]{2,1,0:T(8,128)(2,1)S(1)}, u32[]{:S(2)}, u32[]{:S(2)}) async-start(bf16[8,32,1920]{2,1,0:T(8,128)(2,1)} %bitcast.128), calls=%async_computation.13 | async-start | bytes 1966080 | tf_op jit(solution)/shard_map/cond/branch_6_fun/all_to_all | solution.py:64
  40.0 14.8 %collective-permute-start.48 = (bf16[192,1152]{1,0:T(8,128)(2,1)S(1)}, bf16[192,1152]{1,0:T(8,128)(2,1)S(1)}, u32[]{:S(2)}, u32[]{:S(2)}) collective-permute-start(bf16[192,1152]{1,0:T(8,128)(2,1)S(1)} %convolution_convert_fusion.26), channel_id=1, source_target_pairs={{0,1},{1,2},{2,3},{3,0},{4,5},{5,6},{6,7},{7,4},{8,9},{9,10},{10,1... | collective-permute-start | bytes 1327112 | tf_op jit(solution)/shard_map/cond/branch_6_fun/ppermute | solution.py:52
  40.1 14.3 %collective-permute-start.45 = (s32[256]{0:T(256)S(1)}, s32[256]{0:T(256)S(1)}, u32[]{:S(2)}, u32[]{:S(2)}) collective-permute-start(s32[256]{0:T(256)S(1)} %convert_reduce_fusion.12), channel_id=1, source_target_pairs={{0,1},{1,2},{2,3},{3,0},{4,5},{5,6},{6,7},{7,4},{8,9},{9,10},{10,1... | collective-permute-start | bytes 3080 | tf_op jit(solution)/shard_map/cond/branch_6_fun/ppermute | solution.py:52

commit v3 on v2

--- a/solution.py
+++ b/solution.py
@@ -6,7 +6,7 @@
 LANES = 128
 
 
-FIRST, SECOND = 5, 3
+FIRST, SECOND = 2, 1
 
 
 def exchange(pair_mask, axis, held, program):

time: 56.5 us -> 56.2 us (level)
  starting transfers between devices: 15.3 us -> 19.8 us
  waiting for transfers between devices: 23.5 us -> 19.1 us
    ppermute x4, starting transfers between devices: 1.83 us -> 5.69 us  [next_section(): return lax.ppermute(x, 'section', onward)]
    ppermute x4, waiting for transfers between devices: 19.3 us -> 15.6 us  [next_section(): return lax.ppermute(x, 'section', onward)]
    ppermute x3, waiting for transfers between devices: 2.38 us -> 1.49 us  [arm(): swap = (lambda x: lax.ppermute(x, axis, route)) if k else lambda x: x]
    ppermute x3, starting transfers between devices: 6.15 us -> 7 us  [arm(): swap = (lambda x: lax.ppermute(x, axis, route)) if k else lambda x: x]
  transfers between devices with their start and end apart: 9 -> 9, of which waited for: 4 -> 5; matrix products, arithmetic and copies ran while one was open for 21% -> 21% of each run, Pallas kernels for 0% -> 0%
where the time goes in v3:
time: 56.2 us; the launch traced here: 55.8 us
  starting transfers between devices  19.8 us (35%)
  waiting for transfers between devices  19.1 us (34%)
  matrix products  6.76 us (12%)
  local copies, waits for them, and re-layouts  5.4 us (10%)
  other arithmetic  2.37 us (4%)
  between operations  1.94 us (3%)
    ppermute x4, waiting for transfers between devices, next_section(): return lax.ppermute(x, 'section', onward)  15.6 us
    all_to_all x2, starting transfers between devices, deal(): lax.all_to_all(packed, 'expert', split_axis=0, concat_axis=0, tiled=True)  7.1 us
    ppermute x3, starting transfers between devices, arm(): swap = (lambda x: lax.ppermute(x, axis, route)) if k else lambda x: x  7 us
    ppermute x4, starting transfers between devices, next_section(): return lax.ppermute(x, 'section', onward)  5.69 us
    dot_general x2, matrix products, rows_times_rows(): lax.dot_general(a, b, (((1,), (1,)), ((), ())), preferred_element_type=jn...  2.61 us
    dot_general x2, matrix products, pick_rows(): jnp.dot(pick, x, preferred_element_type=jnp.float32).astype(jnp.bfloat16)  2.55 us
    another operation x2, local copies, waits for them, and re-layouts  1.96 us
    all_to_all x2, waiting for transfers between devices, deal(): lax.all_to_all(packed, 'expert', split_axis=0, concat_axis=0, tiled=True)  1.96 us
  transfers between devices with their start and end apart: 9, of which 5 were waited for; matrix products, arithmetic and copies ran while one was open for 21% of the time, Pallas kernels for 0%

profile of v3, /device:TPU:0, one launch (start us, length us, event | category | flops | bytes accessed | tf_op | source)
XLA Modules:
  0.0 55.8 jit_solution(2388613821610022080)
XLA Ops:
  1.3 0.8 %dynamic-slice_bitcast_fusion = bf16[8,3072]{1,0:T(8,128)(2,1)S(1)} fusion(bf16[1,32,8,3072]{3,2,1,0:T(8,128)(2,1)} %param.19, s32[]{:T(128)S(6)} %select_n.138), kind=kLoop, calls=%fused_computation.442 | loop fusion | bytes 98308 | tf_op jit(solution)/shard_map/jit(dynamic_index_in_dim)/squeeze | solution.py:105
  2.1 0.7 %dynamic-slice_bitcast_fusion.1 = bf16[4,3072]{1,0:T(4,128)(2,1)S(1)} fusion(bf16[1,32,4,3072]{3,2,1,0:T(4,128)(2,1)} %param.20, s32[]{:T(128)S(6)} %select_n.138), kind=kLoop, calls=%fused_computation.443 | loop fusion | bytes 49156 | tf_op jit(solution)/shard_map/jit(dynamic_index_in_dim)/squeeze | solution.py:106
  3.5 52.3 %conditional.1 = (bf16[1,192,3072]{2,1,0:T(8,128)(2,1)}, f32[1,12,3072]{2,0,1:T(1,128)}, f32[1,12,3072]{2,0,1:T(1,128)}) conditional(s32[]{:T(128)} %bitcast.133, (s32[1,128]{1,0:T(1,128)}, f32[1,128]{1,0:T(1,128)}, bf16[12,3072]{1,0:T(8,128)(2,1)S(1)}, s32[]{:T(128)}, bf16[1,32,8,3072]{3,2,1,0:T(8,128)(2,1)}, ...), branch_computations={%region_0.2_spmd, %region_2.4_spmd, %region_4.6_spmd, %region_6.8_... | conditional | flops 929849152 | bytes 38479360 | solution.py:26
  3.7 4.0 %collective-permute-start.35 = (bf16[12,3072]{1,0:T(8,128)(2,1)S(1)}, bf16[12,3072]{1,0:T(8,128)(2,1)S(1)}, u32[]{:S(2)}, u32[]{:S(2)}) collective-permute-start(bf16[12,3072]{1,0:T(8,128)(2,1)S(1)} %get-tuple-element.232), channel_id=1, source_target_pairs={{0,24},{4,28},{8,16},{12,20},{16,8},{20,12},{24,0},{28,4},{1,25},{... | collective-permute-start | bytes 221192 | tf_op jit(solution)/shard_map/cond/branch_5_fun/ppermute | solution.py:22
  7.7 0.9 %copy.186 = f32[1,12,3072]{2,1,0:T(8,128)S(1)} copy(f32[1,12,3072]{2,0,1:T(1,128)} %get-tuple-element.653) | data formatting | bytes 294912 | tf_op jit(solution)/shard_map
  8.6 0.1 collective-permute-start.36
  8.7 0.0 copy-start.12
  8.7 1.0 %copy.185 = f32[1,12,3072]{2,1,0:T(8,128)S(1)} copy(f32[1,12,3072]{2,0,1:T(1,128)} %get-tuple-element.654) | data formatting | bytes 294912 | tf_op jit(solution)/shard_map
  9.8 3.0 %collective-permute-start.37 = (f32[12,1,3072]{2,0,1:T(8,128)S(1)}, f32[12,1,3072]{2,0,1:T(8,128)S(1)}, u32[]{:S(2)}, u32[]{:S(2)}) collective-permute-start(f32[12,1,3072]{2,0,1:T(8,128)S(1)} %bitcast.350), channel_id=1, source_target_pairs={{0,24},{4,28},{8,16},{12,20},{16,8},{20,12},{24,0},{28,4},{1,25},{... | collective-permute-start | bytes 442376 | tf_op jit(solution)/shard_map/cond/branch_5_fun/ppermute | solution.py:22
  12.7 2.3 %fusion.202 = f32[128,256]{1,0:T(8,128)S(1)} fusion(bf16[1,32,8,3072]{3,2,1,0:T(8,128)(2,1)} %get-tuple-element.235, bf16[1,128,3072]{2,1,0:T(8,128)(2,1)} %get-tuple-element.361), kind=kOutput, calls=%fused_computation.320 | convolution fusion | flops 201326592 | bytes 2490368 | tf_op jit(solution)/shard_map/cond/branch_5_fun/dot_general | solution.py:33
  15.0 0.0 copy-start.5
  15.0 0.1 slice.242
  15.1 0.7 %compare_and_fusion.5 = pred[256]{0:T(512)(128)(4,1)S(1)} fusion(s32[]{:T(128)} %get-tuple-element.233), kind=kLoop, calls=%fused_computation.361 | loop fusion | flops 3840 | bytes 260 | tf_op jit(solution)/shard_map/cond/branch_5_fun/and | solution.py:73
  15.9 0.0 copy-done.26
  15.9 0.1 convert_reduce_fusion.11
  16.0 0.0 copy-done.12
  16.0 0.4 fusion.200
  16.4 0.0 copy-start.19
  16.5 0.0 collective-permute-done.35
  16.5 0.0 copy-done.5
  16.5 0.3 convolution_bitcast_fusion.5
  16.8 0.4 fusion.227
  17.2 0.0 copy-done.19
  17.2 0.3 multiply_convert_fusion.5
  17.6 0.0 copy-start.33
  17.6 1.0 %collective-permute-start.40 = (bf16[128,2048]{1,0:T(8,128)(2,1)S(1)}, bf16[128,2048]{1,0:T(8,128)(2,1)S(1)}, u32[]{:S(2)}, u32[]{:S(2)}) collective-permute-start(bf16[128,2048]{1,0:T(8,128)(2,1)S(1)} %slice.244), channel_id=1, source_target_pairs={{0,1},{1,2},{2,3},{3,0},{4,5},{5,6},{6,7},{7,4},{8,9},{9,10},{10,1... | collective-permute-start | bytes 1572872 | tf_op jit(solution)/shard_map/cond/branch_5_fun/ppermute | solution.py:52
  18.7 0.0 collective-permute-done.36
  18.7 1.5 %collective-permute-done.37 = f32[12,1,3072]{2,0,1:T(8,128)S(1)} collective-permute-done((f32[12,1,3072]{2,0,1:T(8,128)S(1)}, f32[12,1,3072]{2,0,1:T(8,128)S(1)}, u32[]{:S(2)}, u32[]{:S(2)}) %collective-permute-start.37) | collective-permute-done | bytes 147488 | tf_op jit(solution)/shard_map/cond/branch_5_fun/ppermute | solution.py:22
  20.2 0.1 broadcast_in_dim.146
  20.3 1.2 %convolution_convert_fusion.21 = bf16[256,1152]{1,0:T(8,128)(2,1)} fusion(bf16[128,128]{1,0:T(8,128)(2,1)S(1)} %broadcast_in_dim.146, bf16[128,1024]{1,0:T(8,128)(2,1)S(1)} %slice.245, s32[128]{0:T(128)S(1)} %get-tuple-element.681), kind=kOutput, calls=%fused_computation.316 | convolution fusion | flops 76414976 | bytes 885248 | tf_op jit(solution)/shard_map/cond/branch_5_fun/dot_general | solution.py:56
  21.4 3.5 %all-to-all-start.10 = ((bf16[8,32,1152]{2,1,0:T(8,128)(2,1)}), bf16[8,32,1152]{2,1,0:T(8,128)(2,1)S(1)}, u32[]{:S(2)}, u32[]{:S(2)}) async-start(bf16[8,32,1152]{2,1,0:T(8,128)(2,1)} %bitcast.107), calls=%async_computation.10 | async-start | bytes 1179648 | tf_op jit(solution)/shard_map/cond/branch_5_fun/all_to_all | solution.py:64
  25.0 1.5 %collective-permute-start.39 = (s32[128]{0:T(128)S(1)}, s32[128]{0:T(128)S(1)}, u32[]{:S(2)}, u32[]{:S(2)}) collective-permute-start(s32[128]{0:T(128)S(1)} %multiply_add_fusion.5), channel_id=1, source_target_pairs={{0,1},{1,2},{2,3},{3,0},{4,5},{5,6},{6,7},{7,4},{8,9},{9,10},{10,1... | collective-permute-start | bytes 1544 | tf_op jit(solution)/shard_map/cond/branch_5_fun/ppermute | solution.py:52
  26.4 7.1 %collective-permute-done.39 = s32[128]{0:T(128)S(1)} collective-permute-done((s32[128]{0:T(128)S(1)}, s32[128]{0:T(128)S(1)}, u32[]{:S(2)}, u32[]{:S(2)}) %collective-permute-start.39) | collective-permute-done | bytes 544 | tf_op jit(solution)/shard_map/cond/branch_5_fun/ppermute | solution.py:52
  33.5 0.0 collective-permute-done.40
  33.5 1.4 %convolution_convert_fusion.20 = bf16[256,2048]{1,0:T(8,128)(2,1)} fusion(bf16[128,2048]{1,0:T(8,128)(2,1)S(1)} %collective-permute-done.40, s32[128]{0:T(128)S(1)} %collective-permute-done.39), kind=kOutput, calls=%fused_computation.315 | convolution fusion | flops 134774784 | bytes 1573376 | tf_op jit(solution)/shard_map/cond/branch_5_fun/dot_general | solution.py:56
  34.9 0.4 all-to-all-done.10
  35.3 3.6 %all-to-all-start.11 = ((bf16[8,32,2048]{2,1,0:T(8,128)(2,1)}), bf16[8,32,2048]{2,1,0:T(8,128)(2,1)S(1)}, u32[]{:S(2)}, u32[]{:S(2)}) async-start(bf16[8,32,2048]{2,1,0:T(8,128)(2,1)} %bitcast.109), calls=%async_computation.11 | async-start | bytes 2097152 | tf_op jit(solution)/shard_map/cond/branch_5_fun/all_to_all | solution.py:64
  38.9 0.1 convert_reduce_fusion.10
  39.0 0.3 convolution_convert_fusion.23
  39.3 1.6 %collective-permute-start.41 = (bf16[192,1024]{1,0:T(8,128)(2,1)S(1)}, bf16[192,1024]{1,0:T(8,128)(2,1)S(1)}, u32[]{:S(2)}, u32[]{:S(2)}) collective-permute-start(bf16[192,1024]{1,0:T(8,128)(2,1)S(1)} %convolution_convert_fusion.23), channel_id=1, source_target_pairs={{0,1},{1,2},{2,3},{3,0},{4,5},{5,6},{6,7},{7,4},{8,9},{9,10},{10,1... | collective-permute-start | bytes 1179656 | tf_op jit(solution)/shard_map/cond/branch_5_fun/ppermute | solution.py:52
  40.9 1.6 %collective-permute-start.38 = (s32[256]{0:T(256)S(1)}, s32[256]{0:T(256)S(1)}, u32[]{:S(2)}, u32[]{:S(2)}) collective-permute-start(s32[256]{0:T(256)S(1)} %convert_reduce_fusion.10), channel_id=1, source_target_pairs={{0,1},{1,2},{2,3},{3,0},{4,5},{5,6},{6,7},{7,4},{8,9},{9,10},{10,1... | collective-permute-start | bytes 3080 | tf_op jit(solution)/shard_map/cond/branch_5_fun/ppermute | solution.py:52
  42.5 0.8 %copy.152 = f32[1,12,3072]{2,0,1:T(1,128)} copy(f32[1,12,3072]{2,1,0:T(8,128)S(1)} %bitcast.329) | data formatting | bytes 294912 | tf_op jit(solution)/shard_map/cond | solution.py:26
  43.4 0.8 %copy.159 = f32[1,12,3072]{2,0,1:T(1,128)} copy(f32[1,12,3072]{2,1,0:T(8,128)S(1)} %bitcast.336) | data formatting | bytes 294912 | tf_op jit(solution)/shard_map/cond | solution.py:26
  44.2 8.5 %collective-permute-done.38 = s32[256]{0:T(256)S(1)} collective-permute-done((s32[256]{0:T(256)S(1)}, s32[256]{0:T(256)S(1)}, u32[]{:S(2)}, u32[]{:S(2)}) %collective-permute-start.38) | collective-permute-done | bytes 1056 | tf_op jit(solution)/shard_map/cond/branch_5_fun/ppermute | solution.py:52
  52.7 1.5 %all-to-all-done.11 = bf16[8,32,2048]{2,1,0:T(8,128)(2,1)S(1)} async-done(((bf16[8,32,2048]{2,1,0:T(8,128)(2,1)}), bf16[8,32,2048]{2,1,0:T(8,128)(2,1)S(1)}, u32[]{:S(2)}, u32[]{:S(2)}) %all-to-all-start.11) | async-done | bytes 1048608 | tf_op jit(solution)/shard_map/cond/branch_5_fun/all_to_all | solution.py:64
  54.2 0.4 convolution_convert_fusion.22
  54.7 0.0 collective-permute-done.41
  54.7 1.1 %maximum_bitcast_fusion.5 = bf16[1,192,3072]{2,1,0:T(8,128)(2,1)} fusion(bf16[192,1024]{1,0:T(8,128)(2,1)S(1)} %collective-permute-done.41, bf16[192,2048]{1,0:T(8,128)(2,1)S(1)} %convolution_convert_fusion.22), kind=kLoop, calls=%fused_computation.325 | loop fusion | flops 2359296 | bytes 2359296 | tf_op jit(solution)/shard_map/cond/branch_5_fun/broadcast_in_dim | solution.py:103
  (9 shorter events, 0.1 us)
Async XLA Ops:
  3.7 12.7 %collective-permute-start.35 = (bf16[12,3072]{1,0:T(8,128)(2,1)S(1)}, bf16[12,3072]{1,0:T(8,128)(2,1)S(1)}, u32[]{:S(2)}, u32[]{:S(2)}) collective-permute-start(bf16[12,3072]{1,0:T(8,128)(2,1)S(1)} %get-tuple-element.232), channel_id=1, source_target_pairs={{0,24},{4,28},{8,16},{12,20},{16,8},{20,12},{24,0},{28,4},{1,25},{... | collective-permute-start | bytes 221192 | tf_op jit(solution)/shard_map/cond/branch_5_fun/ppermute | solution.py:22
  8.6 10.0 %collective-permute-start.36 = (f32[12,1,3072]{2,0,1:T(8,128)S(1)}, f32[12,1,3072]{2,0,1:T(8,128)S(1)}, u32[]{:S(2)}, u32[]{:S(2)}) collective-permute-start(f32[12,1,3072]{2,0,1:T(8,128)S(1)} %bitcast.343), channel_id=1, source_target_pairs={{0,24},{4,28},{8,16},{12,20},{16,8},{20,12},{24,0},{28,4},{1,25},{... | collective-permute-start | bytes 442376 | tf_op jit(solution)/shard_map/cond/branch_5_fun/ppermute | solution.py:22
  8.7 7.2 %copy-start.26 = (s32[1,128]{1,0:T(1,128)S(1)}, s32[1,128]{1,0:T(1,128)}, u32[]{:S(2)}) copy-start(s32[1,128]{1,0:T(1,128)} %get-tuple-element.319) | copy-start | bytes 1540 | tf_op jit(solution)/shard_map/cond
  8.7 7.3 %copy-start.12 = (bf16[1,32,4,3072]{3,2,1,0:T(4,128)(2,1)S(1)}, bf16[1,32,4,3072]{3,2,1,0:T(4,128)(2,1)}, u32[]{:S(2)}) copy-start(bf16[1,32,4,3072]{3,2,1,0:T(4,128)(2,1)} %get-tuple-element.236) | copy-start | bytes 2359300 | tf_op jit(solution)/shard_map/cond
  9.8 10.4 %collective-permute-start.37 = (f32[12,1,3072]{2,0,1:T(8,128)S(1)}, f32[12,1,3072]{2,0,1:T(8,128)S(1)}, u32[]{:S(2)}, u32[]{:S(2)}) collective-permute-start(f32[12,1,3072]{2,0,1:T(8,128)S(1)} %bitcast.350), channel_id=1, source_target_pairs={{0,24},{4,28},{8,16},{12,20},{16,8},{20,12},{24,0},{28,4},{1,25},{... | collective-permute-start | bytes 442376 | tf_op jit(solution)/shard_map/cond/branch_5_fun/ppermute | solution.py:22
  15.0 1.4 %copy-start.5 = (bf16[1,128,3072]{2,1,0:T(8,128)(2,1)S(1)}, bf16[1,128,3072]{2,1,0:T(8,128)(2,1)}, u32[]{:S(2)}) copy-start(bf16[1,128,3072]{2,1,0:T(8,128)(2,1)} %get-tuple-element.361) | copy-start | bytes 2359300 | tf_op jit(solution)/shard_map/cond
  16.4 0.8 %copy-start.19 = (f32[1,128]{1,0:T(1,128)S(1)}, f32[1,128]{1,0:T(1,128)}, u32[]{:S(2)}) copy-start(f32[1,128]{1,0:T(1,128)} %get-tuple-element.326) | copy-start | bytes 1540 | tf_op jit(solution)/shard_map/cond
  17.6 1.1 %copy-start.33 = (s32[1,128]{1,0:T(1,128)S(1)}, s32[1,128]{1,0:T(1,128)}, u32[]{:S(2)}) copy-start(s32[1,128]{1,0:T(1,128)} %get-tuple-element.354) | copy-start | bytes 1540 | tf_op jit(solution)/shard_map/cond
  17.6 15.9 %collective-permute-start.40 = (bf16[128,2048]{1,0:T(8,128)(2,1)S(1)}, bf16[128,2048]{1,0:T(8,128)(2,1)S(1)}, u32[]{:S(2)}, u32[]{:S(2)}) collective-permute-start(bf16[128,2048]{1,0:T(8,128)(2,1)S(1)} %slice.244), channel_id=1, source_target_pairs={{0,1},{1,2},{2,3},{3,0},{4,5},{5,6},{6,7},{7,4},{8,9},{9,10},{10,1... | collective-permute-start | bytes 1572872 | tf_op jit(solution)/shard_map/cond/branch_5_fun/ppermute | solution.py:52
  21.4 13.9 %all-to-all-start.10 = ((bf16[8,32,1152]{2,1,0:T(8,128)(2,1)}), bf16[8,32,1152]{2,1,0:T(8,128)(2,1)S(1)}, u32[]{:S(2)}, u32[]{:S(2)}) async-start(bf16[8,32,1152]{2,1,0:T(8,128)(2,1)} %bitcast.107), calls=%async_computation.10 | async-start | bytes 1179648 | tf_op jit(solution)/shard_map/cond/branch_5_fun/all_to_all | solution.py:64
  25.0 8.6 %collective-permute-start.39 = (s32[128]{0:T(128)S(1)}, s32[128]{0:T(128)S(1)}, u32[]{:S(2)}, u32[]{:S(2)}) collective-permute-start(s32[128]{0:T(128)S(1)} %multiply_add_fusion.5), channel_id=1, source_target_pairs={{0,1},{1,2},{2,3},{3,0},{4,5},{5,6},{6,7},{7,4},{8,9},{9,10},{10,1... | collective-permute-start | bytes 1544 | tf_op jit(solution)/shard_map/cond/branch_5_fun/ppermute | solution.py:52
  35.3 18.9 %all-to-all-start.11 = ((bf16[8,32,2048]{2,1,0:T(8,128)(2,1)}), bf16[8,32,2048]{2,1,0:T(8,128)(2,1)S(1)}, u32[]{:S(2)}, u32[]{:S(2)}) async-start(bf16[8,32,2048]{2,1,0:T(8,128)(2,1)} %bitcast.109), calls=%async_computation.11 | async-start | bytes 2097152 | tf_op jit(solution)/shard_map/cond/branch_5_fun/all_to_all | solution.py:64
  39.3 15.3 %collective-permute-start.41 = (bf16[192,1024]{1,0:T(8,128)(2,1)S(1)}, bf16[192,1024]{1,0:T(8,128)(2,1)S(1)}, u32[]{:S(2)}, u32[]{:S(2)}) collective-permute-start(bf16[192,1024]{1,0:T(8,128)(2,1)S(1)} %convolution_convert_fusion.23), channel_id=1, source_target_pairs={{0,1},{1,2},{2,3},{3,0},{4,5},{5,6},{6,7},{7,4},{8,9},{9,10},{10,1... | collective-permute-start | bytes 1179656 | tf_op jit(solution)/shard_map/cond/branch_5_fun/ppermute | solution.py:52
  40.9 11.8 %collective-permute-start.38 = (s32[256]{0:T(256)S(1)}, s32[256]{0:T(256)S(1)}, u32[]{:S(2)}, u32[]{:S(2)}) collective-permute-start(s32[256]{0:T(256)S(1)} %convert_reduce_fusion.10), channel_id=1, source_target_pairs={{0,1},{1,2},{2,3},{3,0},{4,5},{5,6},{6,7},{7,4},{8,9},{9,10},{10,1... | collective-permute-start | bytes 3080 | tf_op jit(solution)/shard_map/cond/branch_5_fun/ppermute | solution.py:52
